TPU v7x, 1024 devices: a whole 8x8x8 slice. The times are simulated.
1024 devices in a mesh: batch: 8 (over x_hi, core), heads: 8 (over z), seq: 16 (over x_lo, y).
Axes of the slice: x: 8 (x_hi: 4, x_lo: 2; x = x_hi * 2 + x_lo), y: 8, z: 8, core: 2. Of those that a mesh axis runs over, the one named last changes fastest.
Arguments:
- tokens: bfloat16 [8, 2048, 1536], P('batch', 'seq'), may hold values from -24 to 24
- conv_taps: float32 [5, 1536], replicated, may hold values from -2.5 to 2.5
- w_query: bfloat16 [1536, 1024], P(None, 'heads')
- w_key: bfloat16 [1536, 1024], P(None, 'heads')
- w_value: bfloat16 [1536, 1536], P(None, 'heads'), may hold values from -0.15625 to 0.15625
- grad_out: bfloat16 [8, 2048, 1536], P('batch', 'seq', 'heads'), may hold values from -4 to 4
Outputs:
- attended: bfloat16 [8, 2048, 1536], P('batch', 'seq', 'heads')
- grad_tokens: float32 [8, 2048, 1536], P('batch', 'seq', 'heads')
- grad_query: float32 [1536, 1024], P(('batch', 'seq'), 'heads')
- grad_key: float32 [1536, 1024], P(('batch', 'seq'), 'heads')
- grad_value: float32 [1536, 1536], P(('batch', 'seq'), 'heads')
All inputs are finite; a program needn't handle non-finite values.
Results may differ from a plain program's by a relative error of at most 0.02.
The roundings to bfloat16 on the way count: a program that leaves them out, or rounds other values in their place, can miss the bound.
Values may be sent and summed in bfloat16 or wider, within the bound.
No kernel may reach another device: no remote copies, remote signals or barrier semaphores. Data moves between devices by JAX's collectives and lax.ppermute only.
A program may use at most 32 MiB of HBM per device.

v0:
```python
import math

import jax
import jax.numpy as jnp
from jax import lax
from jax.sharding import PartitionSpec as P

DH = 128
DV = 192
DILATION_STEP = 4


def extended(block, sides, width):
    for axis, dim in sides:
        count = lax.axis_size(axis)
        forward = [(i, i + 1) for i in range(count - 1)]
        backward = [(target, source) for source, target in forward]
        low = lax.ppermute(
            lax.slice_in_dim(block, block.shape[dim] - width, None, axis=dim), axis, forward
        )
        high = lax.ppermute(lax.slice_in_dim(block, 0, width, axis=dim), axis, backward)
        block = jnp.concatenate([low, block, high], axis=dim)
    return block


def dilated(signal, kernel, shift_direction):
    border_rows = 2 * DILATION_STEP
    length = signal.shape[0]
    padded = extended(signal, (("seq", 0),), border_rows)
    summed = signal.astype(jnp.float32)
    for kernel_tap_index in range(5):
        tap_offset = shift_direction * DILATION_STEP * (kernel_tap_index - 2)
        summed = summed + kernel[kernel_tap_index] * padded[
            border_rows + tap_offset : border_rows + tap_offset + length
        ].astype(jnp.float32)
    return summed


def local(tokens, conv_taps, w_query, w_key, w_value, grad_out):
    local_rows = tokens.shape[1]
    feature_columns = tokens.shape[2]
    head_count = w_query.shape[1] // DH
    blended = dilated(tokens[0], conv_taps, 1).astype(jnp.bfloat16)
    queries = jnp.dot(blended, w_query, preferred_element_type=jnp.float32).astype(jnp.bfloat16)
    key_rows = jnp.dot(blended, w_key, preferred_element_type=jnp.float32).astype(jnp.bfloat16)
    value_rows = jnp.dot(blended, w_value, preferred_element_type=jnp.float32).astype(jnp.bfloat16)
    all_keys, all_values = (
        lax.all_gather(key_rows, "seq", axis=0, tiled=True),
        lax.all_gather(value_rows, "seq", axis=0, tiled=True),
    )
    total_rows = all_keys.shape[0]
    query_heads = queries.reshape(local_rows, head_count, DH)
    key_heads = all_keys.reshape(total_rows, head_count, DH)
    value_heads = all_values.reshape(total_rows, head_count, DV)
    out_grads = grad_out[0].reshape(local_rows, head_count, DV)
    score_scale = 1.0 / math.sqrt(DH)
    logits = (
        jnp.einsum("qhd,khd->hqk", query_heads, key_heads, preferred_element_type=jnp.float32)
        * score_scale
    )
    exponents = jnp.exp(logits - jnp.max(logits, axis=2, keepdims=True))
    attention = exponents / jnp.sum(exponents, axis=2, keepdims=True)
    attention_b = attention.astype(jnp.bfloat16)
    attended = jnp.einsum(
        "hqk,khe->qhe", attention_b, value_heads, preferred_element_type=jnp.float32
    )
    attended = attended.astype(jnp.bfloat16).reshape(local_rows, head_count * DV)
    attention_grads = jnp.einsum(
        "qhe,khe->hqk", out_grads, value_heads, preferred_element_type=jnp.float32
    )
    row_dots = jnp.sum(attention * attention_grads, axis=2, keepdims=True)
    logit_grads = (attention * (attention_grads - row_dots) * score_scale).astype(jnp.bfloat16)
    query_grads = jnp.einsum(
        "hqk,khd->qhd", logit_grads, key_heads, preferred_element_type=jnp.float32
    )
    query_grads = query_grads.astype(jnp.bfloat16).reshape(local_rows, head_count * DH)
    key_part = jnp.einsum(
        "hqk,qhd->khd", logit_grads, query_heads, preferred_element_type=jnp.float32
    )
    value_part = jnp.einsum(
        "hqk,qhe->khe", attention_b, out_grads, preferred_element_type=jnp.float32
    )
    both_grads = lax.psum_scatter(
        jnp.concatenate(
            (
                key_part.reshape(local_rows * lax.axis_size("seq"), head_count * DH),
                value_part.reshape(local_rows * lax.axis_size("seq"), head_count * DV),
            ),
            axis=1,
        ).astype(jnp.bfloat16),
        "seq",
        scatter_dimension=0,
        tiled=True,
    )
    key_grads = both_grads[:, : head_count * DH]
    value_grads = both_grads[:, head_count * DH :]
    feature_slice = jnp.einsum(
        "sj,cj->sc", query_grads, w_query, preferred_element_type=jnp.float32
    )
    feature_slice = feature_slice + jnp.einsum(
        "sj,cj->sc", key_grads, w_key, preferred_element_type=jnp.float32
    )
    feature_slice = feature_slice + jnp.einsum(
        "sj,cj->sc", value_grads, w_value, preferred_element_type=jnp.float32
    )
    feature_grads = lax.psum_scatter(
        feature_slice.astype(jnp.bfloat16), "heads", scatter_dimension=1, tiled=True
    )
    slice_width = feature_grads.shape[1]
    kernel_part = lax.dynamic_slice_in_dim(
        conv_taps, lax.axis_index("heads") * slice_width, slice_width, 1
    )
    grad_tokens = dilated(feature_grads, kernel_part, -1)
    batch_count = lax.axis_size("batch")
    cycle_count = lax.axis_size("seq")
    grad_scale = 1.0 / math.sqrt(batch_count * cycle_count * local_rows)
    row_share = feature_columns // (batch_count * cycle_count)
    arranged = blended.reshape(local_rows, batch_count, cycle_count, row_share)
    columns = lax.all_to_all(arranged, "seq", split_axis=2, concat_axis=0, tiled=True)
    columns = columns.reshape(total_rows, batch_count * row_share)
    all_query, all_key, all_value = (
        lax.all_gather(query_grads, "seq", axis=0, tiled=True),
        lax.all_gather(key_grads, "seq", axis=0, tiled=True),
        lax.all_gather(value_grads, "seq", axis=0, tiled=True),
    )
    partials = (
        jnp.einsum("pc,pj->cj", columns, all_query, preferred_element_type=jnp.float32),
        jnp.einsum("pc,pj->cj", columns, all_key, preferred_element_type=jnp.float32),
        jnp.einsum("pc,pj->cj", columns, all_value, preferred_element_type=jnp.float32),
    )
    grad_query, grad_key, grad_value = (
        lax.psum_scatter(
            partials[0].astype(jnp.bfloat16), "batch", scatter_dimension=0, tiled=True
        ).astype(jnp.float32),
        lax.psum_scatter(
            partials[1].astype(jnp.bfloat16), "batch", scatter_dimension=0, tiled=True
        ).astype(jnp.float32),
        lax.psum_scatter(
            partials[2].astype(jnp.bfloat16), "batch", scatter_dimension=0, tiled=True
        ).astype(jnp.float32),
    )
    return (
        attended[None],
        grad_tokens[None],
        grad_query * grad_scale,
        grad_key * grad_scale,
        grad_value * grad_scale,
    )


def solution(mesh):
    return jax.shard_map(
        local,
        mesh=mesh,
        in_specs=(
            P("batch", "seq", None),
            P(),
            P(None, "heads"),
            P(None, "heads"),
            P(None, "heads"),
            P("batch", "seq", "heads"),
        ),
        out_specs=(
            P("batch", "seq", "heads"),
            P("batch", "seq", "heads"),
            P(("batch", "seq"), "heads"),
            P(("batch", "seq"), "heads"),
            P(("batch", "seq"), "heads"),
        ),
        check_vma=False,
    )
```

profile of v0, /device:TPU:10, one launch (start us, length us, event | category | flops | bytes accessed | tf_op | source)
XLA Modules:
  0.0 322.9 jit_solution(15329162450497169601)
XLA Ops:
  7.2 0.9 slice_bitcast_fusion.1
  8.1 3.6 %collective-permute-start = (bf16[8,1536]{1,0:T(8,128)(2,1)S(1)}, bf16[8,1536]{1,0:T(8,128)(2,1)S(1)}, u32[]{:S(2)}, u32[]{:S(2)}) collective-permute-start(bf16[8,1536]{1,0:T(8,128)(2,1)S(1)} %get-tuple-element.16), channel_id=1, source_target_pairs={{0,1},{1,2},{2,3},{3,4},{4,5},{5,6},{6,7},{7,8},{8,9},{9,10},{10,1... | collective-permute-start | bytes 73736 | tf_op jit(solution)/shard_map/ppermute | solution.py:18
  11.7 5.4 %collective-permute-start.1 = (bf16[8,1536]{1,0:T(8,128)(2,1)S(1)}, bf16[8,1536]{1,0:T(8,128)(2,1)S(1)}, u32[]{:S(2)}, u32[]{:S(2)}) collective-permute-start(bf16[8,1536]{1,0:T(8,128)(2,1)S(1)} %get-tuple-element.17), channel_id=1, source_target_pairs={{1,0},{2,1},{3,2},{4,3},{5,4},{6,5},{7,6},{8,7},{9,8},{10,9},{11,1... | collective-permute-start | bytes 73736 | tf_op jit(solution)/shard_map/ppermute | solution.py:21
  17.1 1.1 slice_reduce_fusion.4
  18.6 2.4 fusion.13
  21.0 1.2 convolution_convert_fusion.7
  22.8 37.1 %all_gather.16 = bf16[2048,128]{1,0:T(8,128)(2,1)S(1)} all-gather(bf16[128,128]{1,0:T(8,128)(2,1)S(1)} %convolution_convert_fusion.6), channel_id=1, replica_groups=mesh['batch'=8,'heads'=8,'seq'=16] {'seq'}, dimensions={0}, use_global_device_ids=true | all-gather | bytes 557056 | tf_op jit(solution)/shard_map/all_gather | solution.py:48
  59.9 34.2 %all_gather.15 = bf16[2048,192]{0,1:T(8,128)(2,1)S(1)} all-gather(bf16[128,192]{0,1:T(8,128)(2,1)S(1)} %convolution_convert_fusion.4), channel_id=1, replica_groups=mesh['batch'=8,'heads'=8,'seq'=16] {'seq'}, dimensions={0}, use_global_device_ids=true | all-gather | bytes 835584 | tf_op jit(solution)/shard_map/all_gather | solution.py:49
  94.8 0.5 convolution_convert_fusion
  95.3 0.5 multiply_reduce_fusion
  96.1 0.8 copy-done.3
  97.4 1.6 copy.20
  99.0 1.3 dynamic-slice.13
  100.9 1.6 constant_dynamic-slice_fusion.2
  102.8 0.9 reshape.93
  103.6 2.0 copy.17
  105.7 4.5 %all-to-all-start = ((bf16[128,8,16,12]{0,1,3,2:T(8,128)(2,1)}), bf16[128,8,16,12]{0,1,3,2:T(8,128)(2,1)S(1)}, u32[]{:S(2)}, u32[]{:S(2)}) async-start(bf16[128,8,16,12]{0,1,3,2:T(8,128)(2,1)} %copy.17), calls=%async_computation.1 | async-start | bytes 786432 | tf_op jit(solution)/shard_map/all_to_all | solution.py:119
  110.6 36.9 %all-gather = bf16[2048,1,128]{0,2,1:T(8,128)(2,1)S(1)} all-gather(bf16[128,1,128]{0,2,1:T(8,128)(2,1)S(1)} %bitcast.92), channel_id=2, replica_groups=mesh['batch'=8,'heads'=8,'seq'=16] {'seq'}, dimensions={0}, use_global_device_ids=true | all-gather | bytes 557056 | tf_op jit(solution)/shard_map/all_gather | solution.py:122
  147.5 1.2 fusion.33
  148.8 0.7 copy-done.7
  149.5 1.1 copy.18
  151.0 32.9 %reduce-scatter.13.cloned.1.call-done = bf16[128,320]{1,0:T(8,128)(2,1)} async-done(((bf16[2048,320]{1,0:T(8,128)(2,1)}), bf16[128,320]{1,0:T(8,128)(2,1)}) %reduce-scatter.13.cloned.1.call-update) | async-done | bytes 81936
  183.9 0.8 slice.116
  184.9 0.9 slice.117
  185.8 34.0 %all_gather.18 = bf16[2048,128]{0,1:T(8,128)(2,1)S(1)} all-gather(bf16[128,128]{0,1:T(8,128)(2,1)S(1)} %copy.22), channel_id=1, replica_groups=mesh['batch'=8,'heads'=8,'seq'=16] {'seq'}, dimensions={0}, use_global_device_ids=true | all-gather | bytes 557056 | tf_op jit(solution)/shard_map/all_gather | solution.py:123
  219.8 35.6 %all_gather.19 = bf16[2048,192]{0,1:T(8,128)(2,1)S(1)} all-gather(bf16[128,192]{0,1:T(8,128)(2,1)S(1)} %copy.23), channel_id=1, replica_groups=mesh['batch'=8,'heads'=8,'seq'=16] {'seq'}, dimensions={0}, use_global_device_ids=true | all-gather | bytes 835584 | tf_op jit(solution)/shard_map/all_gather | solution.py:124
  255.8 0.4 fusion.36
  256.2 1.0 fusion.4
  257.6 15.4 %fusion.40 = (bf16[16,128]{1,0:T(8,128)(2,1)S(1)}, bf16[16,128]{1,0:T(8,128)(2,1)S(1)}, bf16[16,192]{1,0:T(8,128)(2,1)S(1)}) fusion(bf16[96,128]{1,0:T(8,128)(2,1)S(1)} %convolution_convert_fusion.9, bf16[96,128]{1,0:T(8,128)(2,1)S(1)} %convolution_convert_fusion.8, bf16[96,192]{1,0:T(8,128)(2,1)S(1)} %convolution_convert_fusion.2), kind=kCustom, calls=%all-reduce-scatter.3 | all-reduce-scatter fusion | flops 57345 | bytes 104448
  273.0 1.9 collective-permute-start.4
  275.0 1.9 collective-permute-start.6
  276.9 1.9 collective-permute-start.7
  278.8 1.9 collective-permute-start.5
  280.8 2.2 fusion.6
  283.0 1.9 collective-permute-start.8
  284.9 1.6 collective-permute-done.5
  286.6 1.9 collective-permute-start.9
  289.1 0.6 convert_multiply_fusion.4
  289.7 0.6 convert_multiply_fusion.3
  290.3 3.9 %collective-permute-done.9 = bf16[12,192]{1,0:T(8,128)(2,1)S(1)} collective-permute-done((bf16[12,192]{1,0:T(8,128)(2,1)S(1)}, bf16[12,192]{1,0:T(8,128)(2,1)S(1)}, u32[]{:S(2)}, u32[]{:S(2)}) %collective-permute-start.9) | collective-permute-done | bytes 4640
  294.4 0.6 convert_multiply_fusion.2
  295.1 4.4 %reduce-scatter.11.cloned.1.call-done = bf16[128,192]{0,1:T(8,128)(2,1)} async-done(((bf16[128,1536]{0,1:T(8,128)(2,1)}), bf16[128,192]{0,1:T(8,128)(2,1)}) %reduce-scatter.11.cloned.1.call-update) | async-done | bytes 49168 | tf_op jit(solution)/shard_map/reduce_scatter | solution.py:106
  299.4 1.0 fusion.41
  300.4 5.8 %collective-permute-start.2 = (bf16[8,192]{0,1:T(8,128)(2,1)S(1)}, bf16[8,192]{0,1:T(8,128)(2,1)S(1)}, u32[]{:S(2)}, u32[]{:S(2)}) collective-permute-start(bf16[8,192]{0,1:T(8,128)(2,1)S(1)} %get-tuple-element.23), channel_id=1, source_target_pairs={{1,0},{2,1},{3,2},{4,3},{5,4},{6,5},{7,6},{8,7},{9,8},{10,9},{11,1... | collective-permute-start | bytes 9224 | tf_op jit(solution)/shard_map/ppermute | solution.py:21
  306.2 1.9 collective-permute-start.3
  308.1 0.8 constant_dynamic-update-slice_fusion.1
  308.9 5.3 %collective-permute-done.3 = bf16[8,192]{0,1:T(8,128)(2,1)S(1)} collective-permute-done((bf16[8,192]{0,1:T(8,128)(2,1)S(1)}, bf16[8,192]{0,1:T(8,128)(2,1)S(1)}, u32[]{:S(2)}, u32[]{:S(2)}) %collective-permute-start.3) | collective-permute-done | bytes 3104 | tf_op jit(solution)/shard_map/ppermute | solution.py:18
  314.3 1.8 fusion.29
  (63 shorter events, 5.3 us)
Async XLA Ops:
  7.2 15.3 %copy-start = (bf16[1536,192]{0,1:T(8,128)(2,1)S(1)}, bf16[1536,192]{0,1:T(8,128)(2,1)}, u32[]{:S(2)}) copy-start(bf16[1536,192]{0,1:T(8,128)(2,1)} %param.10) | copy-start | bytes 1769476
  7.2 15.0 %copy-start.5 = (bf16[1536,128]{1,0:T(8,128)(2,1)S(1)}, bf16[1536,128]{1,0:T(8,128)(2,1)}, u32[]{:S(2)}) copy-start(bf16[1536,128]{1,0:T(8,128)(2,1)} %param.9) | copy-start | bytes 1179652
  7.2 176.7 %reduce-scatter.13.cloned.1.call-start = ((), (), s32[]{:S(2)}) async-start(), calls=%async_computation.4 | async-start | bytes 1671168
  8.1 10.1 %collective-permute-start = (bf16[8,1536]{1,0:T(8,128)(2,1)S(1)}, bf16[8,1536]{1,0:T(8,128)(2,1)S(1)}, u32[]{:S(2)}, u32[]{:S(2)}) collective-permute-start(bf16[8,1536]{1,0:T(8,128)(2,1)S(1)} %get-tuple-element.16), channel_id=1, source_target_pairs={{0,1},{1,2},{2,3},{3,4},{4,5},{5,6},{6,7},{7,8},{8,9},{9,10},{10,1... | collective-permute-start | bytes 73736 | tf_op jit(solution)/shard_map/ppermute | solution.py:18
  11.7 6.9 %collective-permute-start.1 = (bf16[8,1536]{1,0:T(8,128)(2,1)S(1)}, bf16[8,1536]{1,0:T(8,128)(2,1)S(1)}, u32[]{:S(2)}, u32[]{:S(2)}) collective-permute-start(bf16[8,1536]{1,0:T(8,128)(2,1)S(1)} %get-tuple-element.17), channel_id=1, source_target_pairs={{1,0},{2,1},{3,2},{4,3},{5,4},{6,5},{7,6},{8,7},{9,8},{10,9},{11,1... | collective-permute-start | bytes 73736 | tf_op jit(solution)/shard_map/ppermute | solution.py:21
  59.9 34.2 %copy-start.1 = (bf16[2048,128]{1,0:T(8,128)(2,1)}, bf16[2048,128]{1,0:T(8,128)(2,1)S(1)}, u32[]{:S(2)}) copy-start(bf16[2048,128]{1,0:T(8,128)(2,1)S(1)} %all_gather.16) | copy-start | bytes 1572868
  59.9 34.9 %copy-start.15 = (bf16[1,128,192]{1,2,0:T(8,128)(2,1)S(1)}, bf16[1,128,192]{1,2,0:T(8,128)(2,1)}, u32[]{:S(2)}) copy-start(bf16[1,128,192]{1,2,0:T(8,128)(2,1)} %param.11) | copy-start | bytes 147460
  94.1 1.2 copy-start.8
  94.8 1.0 copy-start.14
  96.1 0.8 copy-start.3
  102.5 7.7 %copy-start.2 = (bf16[2048,128]{1,0:T(8,128)(2,1)S(1)}, bf16[2048,128]{1,0:T(8,128)(2,1)}, u32[]{:S(2)}) copy-start(bf16[2048,128]{1,0:T(8,128)(2,1)} %copy-done.1) | copy-start | bytes 1572868
  102.5 7.7 %copy-start.4 = (bf16[128,2048]{1,0:T(8,128)(2,1)S(1)}, bf16[128,2048]{1,0:T(8,128)(2,1)}, u32[]{:S(2)}) copy-start(bf16[128,2048]{1,0:T(8,128)(2,1)} %copy-done.3) | copy-start | bytes 1572868
  105.7 43.1 %all-to-all-start = ((bf16[128,8,16,12]{0,1,3,2:T(8,128)(2,1)}), bf16[128,8,16,12]{0,1,3,2:T(8,128)(2,1)S(1)}, u32[]{:S(2)}, u32[]{:S(2)}) async-start(bf16[128,8,16,12]{0,1,3,2:T(8,128)(2,1)} %copy.17), calls=%async_computation.1 | async-start | bytes 786432 | tf_op jit(solution)/shard_map/all_to_all | solution.py:119
  110.1 189.3 %reduce-scatter.11.cloned.1.call-start = ((), (), s32[]{:S(2)}) async-start(), calls=%async_computation.3 | async-start | bytes 442368 | tf_op jit(solution)/shard_map/reduce_scatter | solution.py:106
  148.8 0.8 copy-start.7
  183.9 71.9 %copy-start.9 = (bf16[128,320]{1,0:T(8,128)(2,1)S(1)}, bf16[128,320]{1,0:T(8,128)(2,1)}, u32[]{:S(2)}) copy-start(bf16[128,320]{1,0:T(8,128)(2,1)} %reduce-scatter.13.cloned.1.call-done) | copy-start | bytes 245764
  219.8 36.4 %copy-start.6 = (bf16[1536,128]{1,0:T(8,128)(2,1)S(1)}, bf16[1536,128]{1,0:T(8,128)(2,1)}, u32[]{:S(2)}) copy-start(bf16[1536,128]{1,0:T(8,128)(2,1)} %param.9) | copy-start | bytes 1179652
  273.0 15.5 %collective-permute-start.4 = (bf16[16,128]{1,0:T(8,128)(2,1)S(1)}, bf16[16,128]{1,0:T(8,128)(2,1)S(1)}, u32[]{:S(2)}, u32[]{:S(2)}) collective-permute-start(bf16[16,128]{1,0:T(8,128)(2,1)S(1)} %get-tuple-element.13), channel_id=1, source_target_pairs={{0,128},{128,256},{256,384},{384,512},{512,640},{640,768},{768,896... | collective-permute-start | bytes 12296
  275.0 39.3 %copy-start.10 = (f32[1,192]{1,0:T(1,128)S(1)}, f32[1,192]{1,0:T(1,128)}, u32[]{:S(2)}) copy-start(f32[1,192]{1,0:T(1,128)} %get-tuple-element.19) | copy-start | bytes 2308
  275.0 39.3 %copy-start.11 = (f32[1,192]{1,0:T(1,128)S(1)}, f32[1,192]{1,0:T(1,128)}, u32[]{:S(2)}) copy-start(f32[1,192]{1,0:T(1,128)} %get-tuple-element.20) | copy-start | bytes 2308
  275.0 39.3 %copy-start.12 = (f32[1,192]{1,0:T(1,128)S(1)}, f32[1,192]{1,0:T(1,128)}, u32[]{:S(2)}) copy-start(f32[1,192]{1,0:T(1,128)} %get-tuple-element.21) | copy-start | bytes 2308
  275.0 39.3 %copy-start.13 = (f32[1,192]{1,0:T(1,128)S(1)}, f32[1,192]{1,0:T(1,128)}, u32[]{:S(2)}) copy-start(f32[1,192]{1,0:T(1,128)} %get-tuple-element.22) | copy-start | bytes 2308
  275.0 13.8 %collective-permute-start.6 = (bf16[16,128]{1,0:T(8,128)(2,1)S(1)}, bf16[16,128]{1,0:T(8,128)(2,1)S(1)}, u32[]{:S(2)}, u32[]{:S(2)}) collective-permute-start(bf16[16,128]{1,0:T(8,128)(2,1)S(1)} %get-tuple-element.14), channel_id=1, source_target_pairs={{0,128},{128,256},{256,384},{384,512},{512,640},{640,768},{768,896... | collective-permute-start | bytes 12296
  276.9 11.8 %collective-permute-start.7 = (bf16[12,128]{1,0:T(8,128)(2,1)S(1)}, bf16[12,128]{1,0:T(8,128)(2,1)S(1)}, u32[]{:S(2)}, u32[]{:S(2)}) collective-permute-start(bf16[12,128]{1,0:T(8,128)(2,1)S(1)} %slice.125), channel_id=1, source_target_pairs={{0,256},{128,384},{256,512},{384,640},{512,768},{640,896},{1,257},... | collective-permute-start | bytes 9224
  278.8 7.7 %collective-permute-start.5 = (bf16[12,128]{1,0:T(8,128)(2,1)S(1)}, bf16[12,128]{1,0:T(8,128)(2,1)S(1)}, u32[]{:S(2)}, u32[]{:S(2)}) collective-permute-start(bf16[12,128]{1,0:T(8,128)(2,1)S(1)} %slice.124), channel_id=1, source_target_pairs={{0,256},{128,384},{256,512},{384,640},{512,768},{640,896},{1,257},... | collective-permute-start | bytes 9224
  283.0 11.2 %collective-permute-start.8 = (bf16[16,192]{1,0:T(8,128)(2,1)S(1)}, bf16[16,192]{1,0:T(8,128)(2,1)S(1)}, u32[]{:S(2)}, u32[]{:S(2)}) collective-permute-start(bf16[16,192]{1,0:T(8,128)(2,1)S(1)} %get-tuple-element.15), channel_id=1, source_target_pairs={{0,128},{128,256},{256,384},{384,512},{512,640},{640,768},{768,896... | collective-permute-start | bytes 18440
  286.6 7.6 %collective-permute-start.9 = (bf16[12,192]{1,0:T(8,128)(2,1)S(1)}, bf16[12,192]{1,0:T(8,128)(2,1)S(1)}, u32[]{:S(2)}, u32[]{:S(2)}) collective-permute-start(bf16[12,192]{1,0:T(8,128)(2,1)S(1)} %slice.126), channel_id=1, source_target_pairs={{0,256},{128,384},{256,512},{384,640},{512,768},{640,896},{1,257},... | collective-permute-start | bytes 13832
  300.4 8.5 %collective-permute-start.2 = (bf16[8,192]{0,1:T(8,128)(2,1)S(1)}, bf16[8,192]{0,1:T(8,128)(2,1)S(1)}, u32[]{:S(2)}, u32[]{:S(2)}) collective-permute-start(bf16[8,192]{0,1:T(8,128)(2,1)S(1)} %get-tuple-element.23), channel_id=1, source_target_pairs={{1,0},{2,1},{3,2},{4,3},{5,4},{6,5},{7,6},{8,7},{9,8},{10,9},{11,1... | collective-permute-start | bytes 9224 | tf_op jit(solution)/shard_map/ppermute | solution.py:21
  306.2 8.1 %collective-permute-start.3 = (bf16[8,192]{0,1:T(8,128)(2,1)S(1)}, bf16[8,192]{0,1:T(8,128)(2,1)S(1)}, u32[]{:S(2)}, u32[]{:S(2)}) collective-permute-start(bf16[8,192]{0,1:T(8,128)(2,1)S(1)} %get-tuple-element.24), channel_id=1, source_target_pairs={{0,1},{1,2},{2,3},{3,4},{4,5},{5,6},{6,7},{7,8},{8,9},{9,10},{10,1... | collective-permute-start | bytes 9224 | tf_op jit(solution)/shard_map/ppermute | solution.py:18
Sparse Core Ops, SparseCore 0:
  99.1 84.7 reduce-scatter.12
  257.4 42.0 reduce-scatter.10
where the time goes:
time: 324 us; the launch traced here: 323 us
  blocking collectives  193 us (60%)
  waiting for transfers between devices  48.6 us (15%)
  starting transfers between devices  32.7 us (10%)
  local copies, waits for them, and re-layouts  16.7 us (5%)
  between operations  15.2 us (5%)
  matrix products  9.71 us (3%)
  other arithmetic  6.91 us (2%)
    unnamed x9, waiting for transfers between devices  38.5 us
    all_gather x1, blocking collectives, local(): lax.all_gather(key_rows, 'seq', axis=0, tiled=True)  37.1 us
    all_gather x1, blocking collectives, local(): lax.all_gather(query_grads, 'seq', axis=0, tiled=True)  36.9 us
    all_gather x1, blocking collectives, local(): lax.all_gather(value_grads, 'seq', axis=0, tiled=True)  35.6 us
    all_gather x1, blocking collectives, local(): lax.all_gather(value_rows, 'seq', axis=0, tiled=True)  34.2 us
    all_gather x1, blocking collectives, local(): lax.all_gather(key_grads, 'seq', axis=0, tiled=True)  34 us
    unnamed x1, blocking collectives  15.4 us
    unnamed x7, starting transfers between devices  11.5 us
  transfers between devices with their start and end apart: 13, of which 6 were waited for; matrix products, arithmetic and copies ran while one was open for 10% of the time, Pallas kernels for 0%

commit v1 on v0

v1 whole, which is shorter than its diff:
```python
import math

import jax
import jax.numpy as jnp
from jax import lax
from jax.experimental import pallas as pl
from jax.experimental.pallas import tpu as pltpu
from jax.sharding import Mesh
from jax.sharding import PartitionSpec as P

DH = 128
DV = 192
DILATION_STEP = 4
REACH = 2 * DILATION_STEP
PAD = 16
VMEM = 16 << 20

F32 = jnp.float32
BF16 = jnp.bfloat16
SEQ = ("sx", "yh", "yl")
QGROUP = ("sx", "yl")
KGROUP = "yh"
PAIR = ("core", "sx")
REST = ("bx", "yh", "yl")


def dot(a, b, ca, cb):
    return lax.dot_general(a, b, (((ca,), (cb,)), ((), ())), preferred_element_type=F32)


def call(body, outs, *args, name):
    def kernel(*refs):
        body(refs[: len(args)], refs[len(args) :])

    return pl.pallas_call(
        kernel,
        out_shape=[jax.ShapeDtypeStruct(s, t) for s, t in outs],
        name=name,
        compiler_params=pltpu.CompilerParams(vmem_limit_bytes=VMEM),
    )(*args)


def exchange(x, axis):
    return lax.all_to_all(x, axis, split_axis=0, concat_axis=0, tiled=True)


def shift_pair(low_source, high_source, axes):
    count = lax.axis_size(axes)
    forward = [(i, i + 1) for i in range(count - 1)]
    backward = [(j, i) for i, j in forward]
    return lax.ppermute(low_source, axes, forward), lax.ppermute(high_source, axes, backward)


def project(ins, outs):
    tokens, low, high, taps, wq, wk, wvt = ins
    blended_out, q_out, kv_out = outs
    rows = tokens.shape[0]
    body = tokens[...].astype(F32)
    padded = jnp.concatenate([low[...].astype(F32), body, high[...].astype(F32)], axis=0)
    summed = body
    for t in range(5):
        summed = summed + taps[t : t + 1, :] * padded[t * DILATION_STEP : t * DILATION_STEP + rows]
    blended = summed.astype(BF16)
    blended_out[...] = blended
    qt = dot(blended, wq[...], 1, 0).T.astype(BF16)
    kt = dot(blended, wk[...], 1, 0).T.astype(BF16)
    vt = dot(wvt[...], blended, 1, 1).astype(BF16)
    for m in range(q_out.shape[0]):
        q_out[m] = qt
    for n in range(kv_out.shape[0]):
        kv_out[n, :DH] = kt
        kv_out[n, DH:] = vt


def lanes(ref, first, last):
    return jnp.concatenate([ref[n, first:last] for n in range(ref.shape[0])], axis=1)


SCALE = 1.0 / math.sqrt(DH)


def statistics(ins, outs):
    kv, q, do = ins
    (stats,) = outs
    k_rows = lanes(kv, 0, DH).T
    v_rows = lanes(kv, DH, DH + DV).T
    width = q.shape[2]
    blocks = q.shape[0]
    for m in range(blocks):
        s = dot(k_rows, q[m], 1, 0) * SCALE
        top = jnp.max(s, axis=0, keepdims=True)
        e = jnp.exp(s - top)
        total = jnp.sum(e, axis=0, keepdims=True)
        dp = dot(v_rows, do[m], 1, 0)
        weighted = jnp.sum(e * dp, axis=0, keepdims=True)
        part = jnp.concatenate([top, total, weighted, jnp.zeros((5, width), F32)], axis=0)
        for c in range(stats.shape[0]):
            stats[c, :, m * width : (m + 1) * width] = part


def attend(ins, outs):
    kv, q, do, stats = ins
    odq, dkv = outs
    kt = lanes(kv, 0, DH)
    vt = lanes(kv, DH, DH + DV)
    k_rows = kt.T
    v_rows = vt.T
    width = q.shape[2]
    dk = dv = None
    for m in range(q.shape[0]):
        part = [stats[c, :, m * width : (m + 1) * width] for c in range(stats.shape[0])]
        top = part[0][0:1]
        for x in part[1:]:
            top = jnp.maximum(top, x[0:1])
        total = jnp.zeros_like(top)
        weighted = jnp.zeros_like(top)
        for x in part:
            factor = jnp.exp(x[0:1] - top)
            total = total + factor * x[1:2]
            weighted = weighted + factor * x[2:3]
        row_dots = weighted / total
        s = dot(k_rows, q[m], 1, 0) * SCALE
        a = jnp.exp(s - top) / total
        ab = a.astype(BF16)
        dp = dot(v_rows, do[m], 1, 0)
        ds = (a * (dp - row_dots) * SCALE).astype(BF16)
        odq[m, :DV] = dot(vt, ab, 1, 0).astype(BF16)
        odq[m, DV:] = dot(kt, ds, 1, 0).astype(BF16)
        dk_m = dot(q[m], ds, 1, 1)
        dv_m = dot(do[m], ab, 1, 1)
        dk = dk_m if dk is None else dk + dk_m
        dv = dv_m if dv is None else dv + dv_m
    for n in range(dkv.shape[0]):
        dkv[n, :DH] = dk[:, n * width : (n + 1) * width].astype(BF16)
        dkv[n, DH:] = dv[:, n * width : (n + 1) * width].astype(BF16)


def add_up(ref):
    total = ref[0].astype(F32)
    for n in range(1, ref.shape[0]):
        total = total + ref[n].astype(F32)
    return total


def features(ins, outs):
    odq, dkv, wq, wk, wv = ins
    attended, grads, feature = outs
    first = add_up(odq)
    second = add_up(dkv).astype(BF16)
    attended[...] = first[:DV].astype(BF16)
    dq = first[DV:].astype(BF16)
    for n in range(grads.shape[0]):
        grads[n, :DH] = dq
        grads[n, DH:] = second
    total = dot(wq[...], dq, 1, 0) + dot(wk[...], second[:DH], 1, 0)
    total = total + dot(wv[...], second[DH:], 1, 0)
    feature[...] = total.astype(BF16)


def outer(ins, outs):
    left, right = ins
    total = dot(left[0], right[0], 1, 1)
    for n in range(1, left.shape[0]):
        total = total + dot(left[n], right[n], 1, 1)
    outs[0][...] = total.astype(BF16)


def weight_sum(ins, outs, scale):
    total = add_up(ins[0]) * scale
    rows = outs[0].shape[0]
    outs[0][...] = total[:rows, :DH]
    outs[1][...] = total[:rows, DH : 2 * DH]
    outs[2][...] = total[:rows, 2 * DH :]


def feature_sum(ins, outs):
    outs[0][...] = add_up(ins[0]).astype(BF16)


def spread(ins, outs):
    own, low, high, taps = ins
    width = own.shape[1]
    body = own[...].astype(F32)
    padded = jnp.concatenate([low[...].astype(F32), body, high[...].astype(F32)], axis=1)
    summed = body
    for t in range(5):
        start = width - (t - 2) * DILATION_STEP
        summed = summed + taps[:, t : t + 1] * padded[:, start : start + width]
    outs[0][...] = summed


def local(tokens, conv_taps, w_query, w_key, w_value, grad_out):
    x = tokens[0]
    rows, columns = x.shape
    q_count = lax.axis_size(QGROUP)
    k_count = lax.axis_size(KGROUP)
    pair_count = lax.axis_size(PAIR)
    bx, core, sx = (lax.axis_size(a) for a in ("bx", "core", "sx"))
    y = lax.axis_size(("yh", "yl"))
    rest = bx * y
    share = columns // (bx * core * sx * y)
    heads = lax.axis_size("heads")
    slice_width = columns // heads

    out_grads = jnp.broadcast_to(grad_out[0].T[None], (q_count, DV, rows))
    do = exchange(out_grads, QGROUP)
    low, high = shift_pair(x[rows - REACH :], x[:REACH], SEQ)
    blended, q_all, kv_all = call(
        project,
        [((rows, columns), BF16), ((q_count, DH, rows), BF16), ((k_count, DH + DV, rows), BF16)],
        x, low, high, conv_taps, w_query, w_key, w_value.T,
        name="project",
    )
    kv = exchange(kv_all, KGROUP)
    q = exchange(q_all, QGROUP)

    groups = blended.reshape(rows, bx, core, sx, y, share)
    groups = jnp.pad(groups, ((0, 0),) * 5 + ((0, PAD - share),))
    groups = groups.transpose(2, 3, 1, 4, 5, 0).reshape(pair_count, rest * PAD, rows)
    left = exchange(groups, PAIR)

    (stats,) = call(
        statistics, [((q_count, 8, q_count * rows), F32)], kv, q, do, name="statistics"
    )
    stats = exchange(stats, QGROUP)
    odq, dkv = call(
        attend,
        [((q_count, DH + DV, rows), BF16), ((k_count, DH + DV, rows), BF16)],
        kv, q, do, stats,
        name="attend",
    )
    dkv = exchange(dkv, KGROUP)
    odq = exchange(odq, QGROUP)
    attended, grads, feature = call(
        features,
        [
            ((DV, rows), BF16),
            ((pair_count, 2 * DH + DV, rows), BF16),
            ((columns, rows), BF16),
        ],
        odq, dkv, w_query, w_key, w_value,
        name="features",
    )
    right = exchange(grads, PAIR)
    feature = exchange(feature.reshape(heads, slice_width, rows), "heads")
    (product,) = call(
        outer, [((rest * PAD, 2 * DH + DV), BF16)], left, right, name="outer"
    )
    product = exchange(product.reshape(rest, PAD, 2 * DH + DV), REST)

    (own,) = call(feature_sum, [((slice_width, rows), BF16)], feature, name="feature_sum")
    before, after = shift_pair(own, own, SEQ)
    taps = lax.dynamic_slice_in_dim(
        conv_taps, lax.axis_index("heads") * slice_width, slice_width, 1
    ).T
    (grad_tokens,) = call(
        spread, [((slice_width, rows), F32)], own, before, after, taps, name="spread"
    )
    scale = 1.0 / math.sqrt(bx * core * sx * y * rows)
    grad_query, grad_key, grad_value = call(
        lambda i, o: weight_sum(i, o, scale),
        [((share, DH), F32), ((share, DH), F32), ((share, DV), F32)],
        product,
        name="weight_sum",
    )
    return attended.T[None], grad_tokens.T[None], grad_query, grad_key, grad_value


def split(mesh):
    batch, heads, seq = mesh.devices.shape
    shape = (batch // 2, 2, heads, 2, seq // 4, 2)
    return Mesh(mesh.devices.reshape(shape), ("bx", "core", "heads", "sx", "yh", "yl"))


def solution(mesh):
    batch = ("bx", "core")
    return jax.shard_map(
        local,
        mesh=split(mesh),
        in_specs=(
            P(batch, SEQ, None),
            P(),
            P(None, "heads"),
            P(None, "heads"),
            P(None, "heads"),
            P(batch, SEQ, "heads"),
        ),
        out_specs=(
            P(batch, SEQ, "heads"),
            P(batch, SEQ, "heads"),
            P(batch + SEQ, "heads"),
            P(batch + SEQ, "heads"),
            P(batch + SEQ, "heads"),
        ),
        check_vma=False,
    )
```

time: 324 us -> 165 us (0.51)
  the two profiles are of different devices: /device:TPU:10 before, /device:TPU:18 now
where the time goes in v1:
time: 165 us; the launch traced here: 164 us
  blocking collectives  62.9 us (38%)
  waiting for transfers between devices  43.1 us (26%)
  starting transfers between devices  41.3 us (25%)
  Pallas kernels  8.74 us (5%)
  local copies, waits for them, and re-layouts  7.44 us (5%)
    all_to_all x6, blocking collectives, exchange(): return lax.all_to_all(x, axis, split_axis=0, concat_axis=0, tiled=True)  62.9 us
    all_to_all x4, waiting for transfers between devices, exchange(): return lax.all_to_all(x, axis, split_axis=0, concat_axis=0, tiled=True)  35.9 us
    all_to_all x4, starting transfers between devices, exchange(): return lax.all_to_all(x, axis, split_axis=0, concat_axis=0, tiled=True)  29.7 us
    pallas_call x8, Pallas kernels, call(): pl.pallas_call(kernel, out_shape=[jax.ShapeDtypeStruct(s, t) for s, t in...  8.74 us
    ppermute x2, starting transfers between devices, shift_pair(): lax.ppermute(low_source, axes, forward)  6.96 us
    ppermute x2, waiting for transfers between devices, shift_pair(): lax.ppermute(high_source, axes, backward)  5.89 us
    unnamed x20, local copies, waits for them, and re-layouts  5.29 us
    ppermute x2, starting transfers between devices, shift_pair(): lax.ppermute(high_source, axes, backward)  4.72 us
  transfers between devices with their start and end apart: 8, of which 7 were waited for; matrix products, arithmetic and copies ran while one was open for 1% of the time, Pallas kernels for 3%

profile of v1, /device:TPU:18, one launch (start us, length us, event | category | flops | bytes accessed | tf_op | source)
XLA Modules:
  0.0 164.3 jit_solution(10148009761724938847)
XLA Ops:
  0.6 0.0 copy-start.7
  0.6 0.8 slice_bitcast_fusion
  1.4 3.6 %collective-permute-start = (bf16[8,1536]{1,0:T(8,128)(2,1)S(1)}, bf16[8,1536]{1,0:T(8,128)(2,1)S(1)}, u32[]{:S(2)}, u32[]{:S(2)}) collective-permute-start(bf16[8,1536]{1,0:T(8,128)(2,1)S(1)} %get-tuple-element.28), channel_id=1, source_target_pairs={{0,1},{1,2},{2,3},{3,4},{4,5},{5,6},{6,7},{7,8},{8,9},{9,10},{10,1... | collective-permute-start | bytes 73736 | tf_op jit(solution)/shard_map/ppermute | solution.py:51
  5.0 2.2 %collective-permute-start.1 = (bf16[8,1536]{1,0:T(8,128)(2,1)S(1)}, bf16[8,1536]{1,0:T(8,128)(2,1)S(1)}, u32[]{:S(2)}, u32[]{:S(2)}) collective-permute-start(bf16[8,1536]{1,0:T(8,128)(2,1)S(1)} %get-tuple-element.27), channel_id=1, source_target_pairs={{1,0},{2,1},{3,2},{4,3},{5,4},{6,5},{7,6},{8,7},{9,8},{10,9},{11,1... | collective-permute-start | bytes 73736 | tf_op jit(solution)/shard_map/ppermute | solution.py:51
  7.3 0.0 collective-permute-done.refs_1_
  7.3 3.5 %collective-permute-done.1.refs_2_ = bf16[8,1536]{1,0:T(8,128)(2,1)S(1)} collective-permute-done((bf16[8,1536]{1,0:T(8,128)(2,1)S(1)}, bf16[8,1536]{1,0:T(8,128)(2,1)S(1)}, u32[]{:S(2)}, u32[]{:S(2)}) %collective-permute-start.1) | collective-permute-done | bytes 24608 | tf_op jit(solution)/shard_map/ppermute | solution.py:51
  10.7 0.0 copy-done.7
  10.7 1.1 copy-done
  11.8 1.0 copy-done.2
  12.8 1.0 copy-done.4
  13.8 1.0 copy-done.6
  14.8 0.8 project.1
  15.6 0.0 copy-start.8
  15.6 16.1 %all_to_all.50.refs_1_ = bf16[4,128,128]{2,1,0:T(8,128)(2,1)S(1)} all-to-all(bf16[4,128,128]{2,1,0:T(8,128)(2,1)S(1)} %get-tuple-element.17), channel_id=1, replica_groups=mesh['bx'=4,'core'=2,'heads'=8,'sx'=2,'yh'=4,'yl'=2] {'sx','yl'}, dimensions={0} | all-to-all | bytes 262144 | tf_op jit(solution)/shard_map/all_to_all | solution.py:44
  31.8 7.8 %all_to_all.51.refs_2_ = bf16[4,192,128]{2,1,0:T(8,128)(2,1)S(1)} all-to-all(bf16[4,192,128]{2,1,0:T(8,128)(2,1)S(1)} %broadcast_in_dim.12), channel_id=1, replica_groups=mesh['bx'=4,'core'=2,'heads'=8,'sx'=2,'yh'=4,'yl'=2] {'sx','yl'}, dimensions={0} | all-to-all | bytes 393216 | tf_op jit(solution)/shard_map/all_to_all | solution.py:44
  39.6 13.0 %all_to_all.52.refs_0_ = bf16[4,320,128]{2,1,0:T(8,128)(2,1)S(1)} all-to-all(bf16[4,320,128]{2,1,0:T(8,128)(2,1)S(1)} %get-tuple-element.16), channel_id=1, replica_groups=mesh['bx'=4,'core'=2,'heads'=8,'sx'=2,'yh'=4,'yl'=2] {'yh'}, dimensions={0} | all-to-all | bytes 655360 | tf_op jit(solution)/shard_map/all_to_all | solution.py:44
  52.6 0.6 statistics.1
  53.2 6.9 %all_to_all.53.refs_3_ = f32[4,8,512]{2,1,0:T(8,128)S(1)} all-to-all(f32[4,8,512]{2,1,0:T(8,128)S(1)} %statistics.1), channel_id=1, replica_groups=mesh['bx'=4,'core'=2,'heads'=8,'sx'=2,'yh'=4,'yl'=2] {'sx','yl'}, dimensions={0} | all-to-all | bytes 131072 | tf_op jit(solution)/shard_map/all_to_all | solution.py:44
  60.1 2.5 %attend.1 = (bf16[4,320,128]{2,1,0:T(8,128)(2,1)S(1)}, bf16[4,320,128]{2,1,0:T(8,128)(2,1)}) custom-call(bf16[4,320,128]{2,1,0:T(8,128)(2,1)S(1)} %all_to_all.52.refs_0_, bf16[4,128,128]{2,1,0:T(8,128)(2,1)S(1)} %all_to_all.50.refs_1_, bf16[4,192,128]{2,1,0:T(8,128)(2,1)S(1)} %all_to_all.51.refs_2_, f32[4,8,512]{2,1,0:T(8,128)S(1)} %all_to_all.53.refs_3_), custom_call_target="tpu_custom_call" | custom-call | tf_op jit(solution)/shard_map/attend/pallas_call | solution.py:35
  62.6 8.6 %all_to_all.54.refs_0_ = bf16[4,320,128]{2,1,0:T(8,128)(2,1)S(1)} all-to-all(bf16[4,320,128]{2,1,0:T(8,128)(2,1)S(1)} %get-tuple-element.18), channel_id=1, replica_groups=mesh['bx'=4,'core'=2,'heads'=8,'sx'=2,'yh'=4,'yl'=2] {'sx','yl'}, dimensions={0} | all-to-all | bytes 655360 | tf_op jit(solution)/shard_map/all_to_all | solution.py:44
  71.2 3.8 %all-to-all-start.5 = ((bf16[4,320,128]{2,1,0:T(8,128)(2,1)}), bf16[4,320,128]{2,1,0:T(8,128)(2,1)S(1)}, u32[]{:S(2)}, u32[]{:S(2)}) async-start(bf16[4,320,128]{2,1,0:T(8,128)(2,1)} %get-tuple-element.19), calls=%async_computation.5 | async-start | bytes 655360 | tf_op jit(solution)/shard_map/all_to_all | solution.py:44
  75.0 0.2 copy.16
  75.2 0.1 reshape.26
  75.3 0.1 pad_bitcast_fusion
  75.4 0.8 copy.17
  76.2 9.0 %all-to-all-done.5.refs_1_ = bf16[4,320,128]{2,1,0:T(8,128)(2,1)S(1)} async-done(((bf16[4,320,128]{2,1,0:T(8,128)(2,1)}), bf16[4,320,128]{2,1,0:T(8,128)(2,1)S(1)}, u32[]{:S(2)}, u32[]{:S(2)}) %all-to-all-start.5) | async-done | bytes 327712 | tf_op jit(solution)/shard_map/all_to_all | solution.py:44
  85.3 4.4 %all-to-all-start.7 = ((bf16[4,512,128]{2,1,0:T(8,128)(2,1)}), bf16[4,512,128]{2,1,0:T(8,128)(2,1)S(1)}, u32[]{:S(2)}, u32[]{:S(2)}) async-start(bf16[4,512,128]{2,1,0:T(8,128)(2,1)} %bitcast.13), calls=%async_computation.7 | async-start | bytes 1048576 | tf_op jit(solution)/shard_map/all_to_all | solution.py:44
  89.7 0.0 copy-done.1
  89.7 0.3 copy.14.refs_4_
  89.9 0.7 copy-done.3
  90.7 0.1 copy-done.5
  90.8 1.3 features.1
  92.1 4.5 %all-to-all-done.7.refs_0_ = bf16[4,512,128]{2,1,0:T(8,128)(2,1)S(1)} async-done(((bf16[4,512,128]{2,1,0:T(8,128)(2,1)}), bf16[4,512,128]{2,1,0:T(8,128)(2,1)S(1)}, u32[]{:S(2)}, u32[]{:S(2)}) %all-to-all-start.7) | async-done | bytes 524320 | tf_op jit(solution)/shard_map/all_to_all | solution.py:44
  96.6 10.5 %all_to_all.55.refs_1_ = bf16[4,448,128]{2,1,0:T(8,128)(2,1)S(1)} all-to-all(bf16[4,448,128]{2,1,0:T(8,128)(2,1)S(1)} %get-tuple-element.23), channel_id=1, replica_groups=mesh['bx'=4,'core'=2,'heads'=8,'sx'=2,'yh'=4,'yl'=2] {'core','sx'}, dimensions={0} | all-to-all | bytes 917504 | tf_op jit(solution)/shard_map/all_to_all | solution.py:44
  107.1 12.9 %all-to-all-start.6 = ((bf16[8,192,128]{2,1,0:T(8,128)(2,1)}), bf16[8,192,128]{2,1,0:T(8,128)(2,1)S(1)}, u32[]{:S(2)}, u32[]{:S(2)}) async-start(bf16[8,192,128]{2,1,0:T(8,128)(2,1)} %bitcast.8), calls=%async_computation.6 | async-start | bytes 786432 | tf_op jit(solution)/shard_map/all_to_all | solution.py:44
  120.0 1.5 outer.1
  121.5 13.5 %all-to-all-done.6.refs_0_ = bf16[8,192,128]{2,1,0:T(8,128)(2,1)S(1)} async-done(((bf16[8,192,128]{2,1,0:T(8,128)(2,1)}), bf16[8,192,128]{2,1,0:T(8,128)(2,1)S(1)}, u32[]{:S(2)}, u32[]{:S(2)}) %all-to-all-start.6) | async-done | bytes 393248 | tf_op jit(solution)/shard_map/all_to_all | solution.py:44
  135.0 8.6 %all-to-all-start.9 = ((bf16[32,16,448]{2,1,0:T(8,128)(2,1)}), bf16[32,16,448]{2,1,0:T(8,128)(2,1)S(1)}, u32[]{:S(2)}, u32[]{:S(2)}) async-start(bf16[32,16,448]{2,1,0:T(8,128)(2,1)} %bitcast.14), calls=%async_computation.9 | async-start | bytes 1048576 | tf_op jit(solution)/shard_map/all_to_all | solution.py:44
  143.6 0.1 feature_sum.1.refs_0_
  143.7 3.4 %collective-permute-start.2 = (bf16[192,128]{1,0:T(8,128)(2,1)S(1)}, bf16[192,128]{1,0:T(8,128)(2,1)S(1)}, u32[]{:S(2)}, u32[]{:S(2)}) collective-permute-start(bf16[192,128]{1,0:T(8,128)(2,1)S(1)} %feature_sum.1.refs_0_), channel_id=1, source_target_pairs={{0,1},{1,2},{2,3},{3,4},{4,5},{5,6},{6,7},{7,8},{8,9},{9,10},{10,1... | collective-permute-start | bytes 147464 | tf_op jit(solution)/shard_map/ppermute | solution.py:51
  147.1 2.5 %collective-permute-start.3 = (bf16[192,128]{1,0:T(8,128)(2,1)S(1)}, bf16[192,128]{1,0:T(8,128)(2,1)S(1)}, u32[]{:S(2)}, u32[]{:S(2)}) collective-permute-start(bf16[192,128]{1,0:T(8,128)(2,1)S(1)} %feature_sum.1.refs_0_), channel_id=1, source_target_pairs={{1,0},{2,1},{3,2},{4,3},{5,4},{6,5},{7,6},{8,7},{9,8},{10,9},{11,1... | collective-permute-start | bytes 147464 | tf_op jit(solution)/shard_map/ppermute | solution.py:51
  149.6 0.1 constant_dynamic-slice_fusion
  149.6 0.1 copy.18
  149.8 1.3 collective-permute-done.2.refs_1_
  151.0 2.4 %collective-permute-done.3.refs_2_ = bf16[192,128]{1,0:T(8,128)(2,1)S(1)} collective-permute-done((bf16[192,128]{1,0:T(8,128)(2,1)S(1)}, bf16[192,128]{1,0:T(8,128)(2,1)S(1)}, u32[]{:S(2)}, u32[]{:S(2)}) %collective-permute-start.3) | collective-permute-done | bytes 49184 | tf_op jit(solution)/shard_map/ppermute | solution.py:51
  153.5 1.2 spread.1
  154.7 8.9 %all-to-all-done.9.refs_0_ = bf16[32,16,448]{2,1,0:T(8,128)(2,1)S(1)} async-done(((bf16[32,16,448]{2,1,0:T(8,128)(2,1)}), bf16[32,16,448]{2,1,0:T(8,128)(2,1)S(1)}, u32[]{:S(2)}, u32[]{:S(2)}) %all-to-all-start.9) | async-done | bytes 458784 | tf_op jit(solution)/shard_map/all_to_all | solution.py:44
  163.6 0.7 weight_sum.1
  (9 shorter events, 0.0 us)
Async XLA Ops:
  0.6 10.1 %copy-start.7 = (f32[5,1536]{1,0:T(8,128)S(1)}, f32[5,1536]{1,0:T(8,128)}, u32[]{:S(2)}) copy-start(f32[5,1536]{1,0:T(8,128)} %refs_3_.2) | copy-start | bytes 92164
  1.4 5.8 %collective-permute-start = (bf16[8,1536]{1,0:T(8,128)(2,1)S(1)}, bf16[8,1536]{1,0:T(8,128)(2,1)S(1)}, u32[]{:S(2)}, u32[]{:S(2)}) collective-permute-start(bf16[8,1536]{1,0:T(8,128)(2,1)S(1)} %get-tuple-element.28), channel_id=1, source_target_pairs={{0,1},{1,2},{2,3},{3,4},{4,5},{5,6},{6,7},{7,8},{8,9},{9,10},{10,1... | collective-permute-start | bytes 73736 | tf_op jit(solution)/shard_map/ppermute | solution.py:51
  5.0 5.7 %collective-permute-start.1 = (bf16[8,1536]{1,0:T(8,128)(2,1)S(1)}, bf16[8,1536]{1,0:T(8,128)(2,1)S(1)}, u32[]{:S(2)}, u32[]{:S(2)}) collective-permute-start(bf16[8,1536]{1,0:T(8,128)(2,1)S(1)} %get-tuple-element.27), channel_id=1, source_target_pairs={{1,0},{2,1},{3,2},{4,3},{5,4},{6,5},{7,6},{8,7},{9,8},{10,9},{11,1... | collective-permute-start | bytes 73736 | tf_op jit(solution)/shard_map/ppermute | solution.py:51
  10.7 1.1 copy-start
  11.8 1.0 copy-start.2
  12.8 1.0 copy-start.4
  13.8 1.0 copy-start.6
  15.6 16.2 %copy-start.8 = (bf16[1,128,192]{1,2,0:T(8,128)(2,1)S(1)}, bf16[1,128,192]{1,2,0:T(8,128)(2,1)}, u32[]{:S(2)}) copy-start(bf16[1,128,192]{1,2,0:T(8,128)(2,1)} %param.11) | copy-start | bytes 147460
  71.2 14.1 %all-to-all-start.5 = ((bf16[4,320,128]{2,1,0:T(8,128)(2,1)}), bf16[4,320,128]{2,1,0:T(8,128)(2,1)S(1)}, u32[]{:S(2)}, u32[]{:S(2)}) async-start(bf16[4,320,128]{2,1,0:T(8,128)(2,1)} %get-tuple-element.19), calls=%async_computation.5 | async-start | bytes 655360 | tf_op jit(solution)/shard_map/all_to_all | solution.py:44
  76.2 13.4 %copy-start.1 = (bf16[1536,192]{0,1:T(8,128)(2,1)S(1)}, bf16[1536,192]{0,1:T(8,128)(2,1)}, u32[]{:S(2)}) copy-start(bf16[1536,192]{0,1:T(8,128)(2,1)} %param.10) | copy-start | bytes 1769476
  85.3 11.4 %all-to-all-start.7 = ((bf16[4,512,128]{2,1,0:T(8,128)(2,1)}), bf16[4,512,128]{2,1,0:T(8,128)(2,1)S(1)}, u32[]{:S(2)}, u32[]{:S(2)}) async-start(bf16[4,512,128]{2,1,0:T(8,128)(2,1)} %bitcast.13), calls=%async_computation.7 | async-start | bytes 1048576 | tf_op jit(solution)/shard_map/all_to_all | solution.py:44
  89.7 1.0 copy-start.3
  89.7 1.1 copy-start.5
  107.1 27.8 %all-to-all-start.6 = ((bf16[8,192,128]{2,1,0:T(8,128)(2,1)}), bf16[8,192,128]{2,1,0:T(8,128)(2,1)S(1)}, u32[]{:S(2)}, u32[]{:S(2)}) async-start(bf16[8,192,128]{2,1,0:T(8,128)(2,1)} %bitcast.8), calls=%async_computation.6 | async-start | bytes 786432 | tf_op jit(solution)/shard_map/all_to_all | solution.py:44
  135.0 28.6 %all-to-all-start.9 = ((bf16[32,16,448]{2,1,0:T(8,128)(2,1)}), bf16[32,16,448]{2,1,0:T(8,128)(2,1)S(1)}, u32[]{:S(2)}, u32[]{:S(2)}) async-start(bf16[32,16,448]{2,1,0:T(8,128)(2,1)} %bitcast.14), calls=%async_computation.9 | async-start | bytes 1048576 | tf_op jit(solution)/shard_map/all_to_all | solution.py:44
  143.7 7.3 %collective-permute-start.2 = (bf16[192,128]{1,0:T(8,128)(2,1)S(1)}, bf16[192,128]{1,0:T(8,128)(2,1)S(1)}, u32[]{:S(2)}, u32[]{:S(2)}) collective-permute-start(bf16[192,128]{1,0:T(8,128)(2,1)S(1)} %feature_sum.1.refs_0_), channel_id=1, source_target_pairs={{0,1},{1,2},{2,3},{3,4},{4,5},{5,6},{6,7},{7,8},{8,9},{9,10},{10,1... | collective-permute-start | bytes 147464 | tf_op jit(solution)/shard_map/ppermute | solution.py:51
  147.1 6.4 %collective-permute-start.3 = (bf16[192,128]{1,0:T(8,128)(2,1)S(1)}, bf16[192,128]{1,0:T(8,128)(2,1)S(1)}, u32[]{:S(2)}, u32[]{:S(2)}) collective-permute-start(bf16[192,128]{1,0:T(8,128)(2,1)S(1)} %feature_sum.1.refs_0_), channel_id=1, source_target_pairs={{1,0},{2,1},{3,2},{4,3},{5,4},{6,5},{7,6},{8,7},{9,8},{10,9},{11,1... | collective-permute-start | bytes 147464 | tf_op jit(solution)/shard_map/ppermute | solution.py:51

commit v2 on v1

v2 whole, which is shorter than its diff:
```python
import math

import jax
import jax.numpy as jnp
from jax import lax
from jax.experimental import pallas as pl
from jax.experimental.pallas import tpu as pltpu
from jax.sharding import Mesh
from jax.sharding import PartitionSpec as P

DH = 128
DV = 192
DILATION_STEP = 4
REACH = 2 * DILATION_STEP
PAD = 16
VMEM = 16 << 20

F32 = jnp.float32
BF16 = jnp.bfloat16
SEQ = ("sx", "yh", "yl")
QGROUP = ("sx", "yl")
KGROUP = "yh"
PAIR = ("core", "sx")
REST = ("bx", "yh", "yl")


def dot(a, b, ca, cb):
    return lax.dot_general(a, b, (((ca,), (cb,)), ((), ())), preferred_element_type=F32)


def call(body, outs, *args, far=0, vmem=VMEM):
    count = len(args)

    def kernel(*refs):
        ins, results = refs[:count], refs[count : count + len(outs)]
        if far:
            held, sems = refs[-1 - far : -1], refs[-1]
            copies = [
                pltpu.make_async_copy(ins[i], held[i], sems.at[i]) for i in range(far)
            ]
            for c in copies:
                c.start()
            body(tuple(held) + ins[far:], results, copies)
        else:
            body(ins, results)

    scratch = [pltpu.VMEM(a.shape, a.dtype) for a in args[:far]]
    if far:
        scratch.append(pltpu.SemaphoreType.DMA((far,)))
    return pl.pallas_call(
        kernel,
        out_shape=[jax.ShapeDtypeStruct(s, t) for s, t in outs],
        in_specs=[pl.BlockSpec(memory_space=pltpu.HBM)] * far
        + [pl.BlockSpec(memory_space=pltpu.VMEM)] * (count - far),
        scratch_shapes=scratch,
        compiler_params=pltpu.CompilerParams(vmem_limit_bytes=vmem),
    )(*args)


def exchange(x, axis):
    return lax.all_to_all(x, axis, split_axis=0, concat_axis=0, tiled=True)


def swap(x, axes, k):
    count = lax.axis_size(axes)
    return lax.ppermute(x, axes, [(i, i ^ k) for i in range(count)])


def gather(x, axes):
    return [x] + [swap(x, axes, k) for k in range(1, lax.axis_size(axes))]


def trade(pieces, axes):
    return [pieces[0]] + [swap(pieces[k], axes, k) for k in range(1, lax.axis_size(axes))]


def shift_pair(low_source, high_source, axes):
    count = lax.axis_size(axes)
    forward = [(i, i + 1) for i in range(count - 1)]
    backward = [(j, i) for i, j in forward]
    return lax.ppermute(low_source, axes, forward), lax.ppermute(high_source, axes, backward)


def project(ins, outs, copies):
    tokens, wq, wk, wvt, low, high, taps = ins
    blended_out, qt, kv_out = outs
    rows = tokens.shape[0]
    copies[0].wait()
    body = tokens[...].astype(F32)
    padded = jnp.concatenate([low[...].astype(F32), body, high[...].astype(F32)], axis=0)
    summed = body
    for t in range(5):
        summed = summed + taps[t : t + 1, :] * padded[t * DILATION_STEP : t * DILATION_STEP + rows]
    blended = summed.astype(BF16)
    blended_out[...] = blended
    copies[1].wait()
    qt[...] = dot(blended, wq[...], 1, 0).T.astype(BF16)
    copies[2].wait()
    kt = dot(blended, wk[...], 1, 0).T.astype(BF16)
    copies[3].wait()
    vt = dot(wvt[...], blended, 1, 1).astype(BF16)
    for n in range(kv_out.shape[0]):
        kv_out[n, :DH] = kt
        kv_out[n, DH:] = vt


def lanes(ref, first, last):
    return jnp.concatenate([ref[n, first:last] for n in range(ref.shape[0])], axis=1)


SCALE = 1.0 / math.sqrt(DH)


def statistics(ins, outs):
    kv, ins = ins[0], ins[1:]
    blocks = len(ins) // 2
    q, do = ins[:blocks], ins[blocks:]
    (stats,) = outs
    k_rows = lanes(kv, 0, DH).T
    v_rows = lanes(kv, DH, DH + DV).T
    width = q[0].shape[1]
    for m in range(blocks):
        s = dot(k_rows, q[m][...], 1, 0) * SCALE
        top = jnp.max(s, axis=0, keepdims=True)
        e = jnp.exp(s - top)
        total = jnp.sum(e, axis=0, keepdims=True)
        dp = dot(v_rows, do[m][...], 1, 0)
        weighted = jnp.sum(e * dp, axis=0, keepdims=True)
        part = jnp.concatenate([top, total, weighted, jnp.zeros((5, width), F32)], axis=0)
        stats[:, m * width : (m + 1) * width] = part


def attend(ins, outs):
    kv, ins = ins[0], ins[1:]
    blocks = len(ins) // 3
    q, do, stats = ins[:blocks], ins[blocks : 2 * blocks], ins[2 * blocks :]
    odq, dkv = outs[:-1], outs[-1]
    kt = lanes(kv, 0, DH)
    vt = lanes(kv, DH, DH + DV)
    k_rows = kt.T
    v_rows = vt.T
    width = q[0].shape[1]
    dk = dv = None
    for m in range(blocks):
        part = [stats[c][:, (m ^ c) * width : ((m ^ c) + 1) * width] for c in range(blocks)]
        top = part[0][0:1]
        for x in part[1:]:
            top = jnp.maximum(top, x[0:1])
        total = jnp.zeros_like(top)
        weighted = jnp.zeros_like(top)
        for x in part:
            factor = jnp.exp(x[0:1] - top)
            total = total + factor * x[1:2]
            weighted = weighted + factor * x[2:3]
        row_dots = weighted / total
        s = dot(k_rows, q[m][...], 1, 0) * SCALE
        a = jnp.exp(s - top) / total
        ab = a.astype(BF16)
        dp = dot(v_rows, do[m][...], 1, 0)
        ds = (a * (dp - row_dots) * SCALE).astype(BF16)
        odq[m][:DV] = dot(vt, ab, 1, 0).astype(BF16)
        odq[m][DV:] = dot(kt, ds, 1, 0).astype(BF16)
        dk_m = dot(q[m][...], ds, 1, 1)
        dv_m = dot(do[m][...], ab, 1, 1)
        dk = dk_m if dk is None else dk + dk_m
        dv = dv_m if dv is None else dv + dv_m
    for n in range(dkv.shape[0]):
        dkv[n, :DH] = dk[:, n * width : (n + 1) * width].astype(BF16)
        dkv[n, DH:] = dv[:, n * width : (n + 1) * width].astype(BF16)


def add_up(pieces):
    total = pieces[0][...].astype(F32)
    for x in pieces[1:]:
        total = total + x[...].astype(F32)
    return total


def planes(ref):
    return [ref.at[n] for n in range(ref.shape[0])]


def features(ins, outs):
    dkv, wq, wk, wv = ins[:4]
    odq = ins[4:]
    attended, grads, feature = outs
    first = add_up(odq)
    second = add_up(planes(dkv)).astype(BF16)
    attended[...] = first[:DV].astype(BF16)
    dq = first[DV:].astype(BF16)
    grads[:DH] = dq
    grads[DH:] = second
    total = dot(wq[...], dq, 1, 0) + dot(wk[...], second[:DH], 1, 0)
    total = total + dot(wv[...], second[DH:], 1, 0)
    feature[...] = total.astype(BF16)


def outer(ins, outs):
    count = len(ins) // 2
    left, right = ins[:count], ins[count:]
    total = dot(left[0][...], right[0][...], 1, 1)
    for n in range(1, count):
        total = total + dot(left[n][...], right[n][...], 1, 1)
    outs[0][...] = total.astype(BF16)


def weight_sum(ins, outs, scale):
    total = add_up(planes(ins[0])) * scale
    rows = outs[0].shape[0]
    outs[0][...] = total[:rows, :DH]
    outs[1][...] = total[:rows, DH : 2 * DH]
    outs[2][...] = total[:rows, 2 * DH :]


def feature_sum(ins, outs):
    outs[0][...] = add_up(planes(ins[0])).astype(BF16)


def spread(ins, outs):
    own, low, high, taps = ins
    width = own.shape[1]
    body = own[...].astype(F32)
    padded = jnp.concatenate([low[...].astype(F32), body, high[...].astype(F32)], axis=1)
    summed = body
    for t in range(5):
        start = width - (t - 2) * DILATION_STEP
        summed = summed + taps[:, t : t + 1] * padded[:, start : start + width]
    outs[0][...] = summed


def local(tokens, conv_taps, w_query, w_key, w_value, grad_out):
    x = tokens[0]
    rows, columns = x.shape
    q_count = lax.axis_size(QGROUP)
    k_count = lax.axis_size(KGROUP)
    pair_count = lax.axis_size(PAIR)
    bx, core, sx = (lax.axis_size(a) for a in ("bx", "core", "sx"))
    y = lax.axis_size(("yh", "yl"))
    rest = bx * y
    share = columns // (bx * core * sx * y)
    heads = lax.axis_size("heads")
    slice_width = columns // heads

    do = gather(grad_out[0].T, QGROUP)
    low, high = shift_pair(x[rows - REACH :], x[:REACH], SEQ)
    low, high, *do = lax.optimization_barrier((low, high, *do))
    blended, qt, kv_all = call(
        project,
        [((rows, columns), BF16), ((DH, rows), BF16), ((k_count, DH + DV, rows), BF16)],
        x, w_query, w_key, w_value.T, low, high, conv_taps,
        far=4, vmem=62 << 20,
    )
    kv = exchange(kv_all, KGROUP)
    q = gather(qt, QGROUP)

    groups = blended.reshape(rows, bx, core, sx, y, share)
    groups = jnp.pad(groups, ((0, 0),) * 5 + ((0, PAD - share),))
    groups = groups.transpose(2, 3, 1, 4, 5, 0).reshape(pair_count, rest * PAD, rows)
    mine = lax.axis_index(PAIR)
    left = trade(
        [lax.dynamic_index_in_dim(groups, mine ^ k, 0, False) for k in range(pair_count)], PAIR
    )

    (stats,) = call(statistics, [((8, q_count * rows), F32)], kv, *q, *do)
    stats = gather(stats, QGROUP)
    *odq, dkv = call(
        attend,
        [((DH + DV, rows), BF16)] * q_count + [((k_count, DH + DV, rows), BF16)],
        kv, *q, *do, *stats,
    )
    dkv = exchange(dkv, KGROUP)
    odq = trade(odq, QGROUP)
    dkv, *left = lax.optimization_barrier((dkv, *left))
    attended, grads, feature = call(
        features,
        [((DV, rows), BF16), ((2 * DH + DV, rows), BF16), ((columns, rows), BF16)],
        dkv, w_query, w_key, w_value, *odq,
    )
    right = gather(grads, PAIR)
    feature = exchange(feature.reshape(heads, slice_width, rows), "heads")
    (product,) = call(outer, [((rest * PAD, 2 * DH + DV), BF16)], *left, *right)
    product = exchange(product.reshape(rest, PAD, 2 * DH + DV), REST)

    (own,) = call(feature_sum, [((slice_width, rows), BF16)], feature)
    before, after = shift_pair(own, own, SEQ)
    taps = lax.dynamic_slice_in_dim(
        conv_taps, lax.axis_index("heads") * slice_width, slice_width, 1
    ).T
    (grad_tokens,) = call(spread, [((slice_width, rows), F32)], own, before, after, taps)
    scale = 1.0 / math.sqrt(bx * core * sx * y * rows)
    grad_query, grad_key, grad_value = call(
        lambda i, o: weight_sum(i, o, scale),
        [((share, DH), F32), ((share, DH), F32), ((share, DV), F32)],
        product,
    )
    return attended.T[None], grad_tokens.T[None], grad_query, grad_key, grad_value


def split(mesh):
    batch, heads, seq = mesh.devices.shape
    shape = (batch // 2, 2, heads, 2, seq // 4, 2)
    return Mesh(mesh.devices.reshape(shape), ("bx", "core", "heads", "sx", "yh", "yl"))


def solution(mesh):
    batch = ("bx", "core")
    whole = split(mesh)
    return jax.shard_map(
        local,
        mesh=whole,
        in_specs=(
            P(batch, SEQ, None),
            P(),
            P(None, "heads"),
            P(None, "heads"),
            P(None, "heads"),
            P(batch, SEQ, "heads"),
        ),
        out_specs=(
            P(batch, SEQ, "heads"),
            P(batch, SEQ, "heads"),
            P(batch + SEQ, "heads"),
            P(batch + SEQ, "heads"),
            P(batch + SEQ, "heads"),
        ),
        check_vma=False,
    )
```

time: 165 us -> 155 us (0.939)
  the two profiles are of different devices: /device:TPU:18 before, /device:TPU:16 now
where the time goes in v2:
time: 155 us; the launch traced here: 154 us
  starting transfers between devices  110 us (71%)
  waiting for transfers between devices  26.2 us (17%)
  Pallas kernels  11.9 us (8%)
  local copies, waits for them, and re-layouts  4.13 us (3%)
    ppermute x18, starting transfers between devices, swap(): return lax.ppermute(x, axes, [(i, i ^ k) for i in range(count)])  63.6 us
    all_to_all x4, starting transfers between devices, exchange(): return lax.all_to_all(x, axis, split_axis=0, concat_axis=0, tiled=True)  34.9 us
    pallas_call x8, Pallas kernels, call(): pl.pallas_call(kernel, out_shape=[jax.ShapeDtypeStruct(s, t) for s, t in...  11.9 us
    ppermute x18, waiting for transfers between devices, swap(): return lax.ppermute(x, axes, [(i, i ^ k) for i in range(count)])  10.8 us
    all_to_all x4, waiting for transfers between devices, exchange(): return lax.all_to_all(x, axis, split_axis=0, concat_axis=0, tiled=True)  10.4 us
    ppermute x2, starting transfers between devices, shift_pair(): lax.ppermute(high_source, axes, backward)  6.39 us
    ppermute x2, starting transfers between devices, shift_pair(): lax.ppermute(low_source, axes, forward)  5.28 us
    ppermute x2, waiting for transfers between devices, shift_pair(): lax.ppermute(high_source, axes, backward)  4.46 us
  transfers between devices with their start and end apart: 26, of which 10 were waited for; matrix products, arithmetic and copies ran while one was open for 2% of the time, Pallas kernels for 2%

profile of v2, /device:TPU:16, one launch (start us, length us, event | category | flops | bytes accessed | tf_op | source)
XLA Modules:
  0.0 153.6 jit_solution(6650405639712889747)
XLA Ops:
  0.6 14.9 %collective-permute-start.2 = (bf16[192,128]{1,0:T(8,128)(2,1)}, bf16[192,128]{1,0:T(8,128)(2,1)S(1)}, u32[]{:S(2)}, u32[]{:S(2)}) collective-permute-start(bf16[192,128]{1,0:T(8,128)(2,1)} %bitcast.32), channel_id=1, source_target_pairs={{0,1},{1,0},{8,9},{9,8},{2,3},{3,2},{10,11},{11,10},{4,5},{5,4},{1... | collective-permute-start | bytes 147464 | tf_op jit(solution)/shard_map/ppermute | solution.py:66
  15.5 1.9 %collective-permute-start.3 = (bf16[192,128]{1,0:T(8,128)(2,1)}, bf16[192,128]{1,0:T(8,128)(2,1)S(1)}, u32[]{:S(2)}, u32[]{:S(2)}) collective-permute-start(bf16[192,128]{1,0:T(8,128)(2,1)} %bitcast.33), channel_id=1, source_target_pairs={{0,8},{1,9},{8,0},{9,1},{2,10},{3,11},{10,2},{11,3},{4,12},{5,13},... | collective-permute-start | bytes 147464 | tf_op jit(solution)/shard_map/ppermute | solution.py:66
  17.4 3.4 %collective-permute-start.4 = (bf16[192,128]{1,0:T(8,128)(2,1)}, bf16[192,128]{1,0:T(8,128)(2,1)S(1)}, u32[]{:S(2)}, u32[]{:S(2)}) collective-permute-start(bf16[192,128]{1,0:T(8,128)(2,1)} %bitcast.34), channel_id=1, source_target_pairs={{0,9},{1,8},{8,1},{9,0},{2,11},{3,10},{10,3},{11,2},{4,13},{5,12},... | collective-permute-start | bytes 147464 | tf_op jit(solution)/shard_map/ppermute | solution.py:66
  20.8 0.8 slice_bitcast_fusion
  21.6 1.9 %collective-permute-start = (bf16[8,1536]{1,0:T(8,128)(2,1)S(1)}, bf16[8,1536]{1,0:T(8,128)(2,1)S(1)}, u32[]{:S(2)}, u32[]{:S(2)}) collective-permute-start(bf16[8,1536]{1,0:T(8,128)(2,1)S(1)} %get-tuple-element.60), channel_id=1, source_target_pairs={{0,1},{1,2},{2,3},{3,4},{4,5},{5,6},{6,7},{7,8},{8,9},{9,10},{10,1... | collective-permute-start | bytes 73736 | tf_op jit(solution)/shard_map/ppermute | solution.py:81
  23.5 3.9 %collective-permute-start.1 = (bf16[8,1536]{1,0:T(8,128)(2,1)S(1)}, bf16[8,1536]{1,0:T(8,128)(2,1)S(1)}, u32[]{:S(2)}, u32[]{:S(2)}) collective-permute-start(bf16[8,1536]{1,0:T(8,128)(2,1)S(1)} %get-tuple-element.59), channel_id=1, source_target_pairs={{1,0},{2,1},{3,2},{4,3},{5,4},{6,5},{7,6},{8,7},{9,8},{10,9},{11,1... | collective-permute-start | bytes 73736 | tf_op jit(solution)/shard_map/ppermute | solution.py:81
  27.4 1.8 %collective-permute-done.1.refs_5_ = bf16[8,1536]{1,0:T(8,128)(2,1)S(1)} collective-permute-done((bf16[8,1536]{1,0:T(8,128)(2,1)S(1)}, bf16[8,1536]{1,0:T(8,128)(2,1)S(1)}, u32[]{:S(2)}, u32[]{:S(2)}) %collective-permute-start.1) | collective-permute-done | bytes 24608 | tf_op jit(solution)/shard_map/ppermute | solution.py:81
  29.2 0.6 copy-done.6
  29.8 4.0 %shard_map.101 = (bf16[128,1536]{1,0:T(8,128)(2,1)}, bf16[128,128]{1,0:T(8,128)(2,1)}, bf16[4,320,128]{2,1,0:T(8,128)(2,1)}) custom-call(bf16[128,1536]{1,0:T(8,128)(2,1)} %bitcast.39, bf16[1536,128]{1,0:T(8,128)(2,1)} %refs_1_.3, bf16[1536,128]{1,0:T(8,128)(2,1)} %refs_2_.3, bf16[192,1536]{1,0:T(8,128)(2,1)} %bitcast.37, bf16[8,1536]{1,0:T(8,128)(2,1)} %copy-done.5, ...), custom_call_target="tpu_custom_call" | custom-call | tf_op jit(solution)/shard_map/pallas_call | solution.py:50
  33.9 7.9 %all-to-all-start = ((bf16[4,320,128]{2,1,0:T(8,128)(2,1)}), bf16[4,320,128]{2,1,0:T(8,128)(2,1)S(1)}, u32[]{:S(2)}, u32[]{:S(2)}) async-start(bf16[4,320,128]{2,1,0:T(8,128)(2,1)} %get-tuple-element.32), calls=%async_computation | async-start | bytes 655360 | tf_op jit(solution)/shard_map/all_to_all | solution.py:61
  41.8 1.9 %collective-permute-start.5 = (bf16[128,128]{1,0:T(8,128)(2,1)S(1)}, bf16[128,128]{1,0:T(8,128)(2,1)S(1)}, u32[]{:S(2)}, u32[]{:S(2)}) collective-permute-start(bf16[128,128]{1,0:T(8,128)(2,1)S(1)} %copy-done.3), channel_id=1, source_target_pairs={{0,1},{1,0},{8,9},{9,8},{2,3},{3,2},{10,11},{11,10},{4,5},{5,4},{1... | collective-permute-start | bytes 98312 | tf_op jit(solution)/shard_map/ppermute | solution.py:66
  43.7 1.9 %collective-permute-start.6 = (bf16[128,128]{1,0:T(8,128)(2,1)S(1)}, bf16[128,128]{1,0:T(8,128)(2,1)S(1)}, u32[]{:S(2)}, u32[]{:S(2)}) collective-permute-start(bf16[128,128]{1,0:T(8,128)(2,1)S(1)} %copy-done.3), channel_id=1, source_target_pairs={{0,8},{1,9},{8,0},{9,1},{2,10},{3,11},{10,2},{11,3},{4,12},{5,13},... | collective-permute-start | bytes 98312 | tf_op jit(solution)/shard_map/ppermute | solution.py:66
  45.7 5.4 %collective-permute-start.7 = (bf16[128,128]{1,0:T(8,128)(2,1)S(1)}, bf16[128,128]{1,0:T(8,128)(2,1)S(1)}, u32[]{:S(2)}, u32[]{:S(2)}) collective-permute-start(bf16[128,128]{1,0:T(8,128)(2,1)S(1)} %copy-done.3), channel_id=1, source_target_pairs={{0,9},{1,8},{8,1},{9,0},{2,11},{3,10},{10,3},{11,2},{4,13},{5,12},... | collective-permute-start | bytes 98312 | tf_op jit(solution)/shard_map/ppermute | solution.py:66
  51.1 1.9 %collective-permute-done.7.refs_4_ = bf16[128,128]{1,0:T(8,128)(2,1)S(1)} collective-permute-done((bf16[128,128]{1,0:T(8,128)(2,1)S(1)}, bf16[128,128]{1,0:T(8,128)(2,1)S(1)}, u32[]{:S(2)}, u32[]{:S(2)}) %collective-permute-start.7) | collective-permute-done | bytes 32800 | tf_op jit(solution)/shard_map/ppermute | solution.py:66
  52.9 0.6 shard_map.102.refs_9_
  53.6 4.8 %collective-permute-start.10 = (f32[8,512]{1,0:T(8,128)S(1)}, f32[8,512]{1,0:T(8,128)S(1)}, u32[]{:S(2)}, u32[]{:S(2)}) collective-permute-start(f32[8,512]{1,0:T(8,128)S(1)} %shard_map.102.refs_9_), channel_id=1, source_target_pairs={{0,9},{1,8},{8,1},{9,0},{2,11},{3,10},{10,3},{11,2},{4,13},{5,12},... | collective-permute-start | bytes 49160 | tf_op jit(solution)/shard_map/ppermute | solution.py:66
  58.4 1.9 %collective-permute-start.8 = (f32[8,512]{1,0:T(8,128)S(1)}, f32[8,512]{1,0:T(8,128)S(1)}, u32[]{:S(2)}, u32[]{:S(2)}) collective-permute-start(f32[8,512]{1,0:T(8,128)S(1)} %shard_map.102.refs_9_), channel_id=1, source_target_pairs={{0,1},{1,0},{8,9},{9,8},{2,3},{3,2},{10,11},{11,10},{4,5},{5,4},{1... | collective-permute-start | bytes 49160 | tf_op jit(solution)/shard_map/ppermute | solution.py:66
  60.3 2.5 %collective-permute-start.9 = (f32[8,512]{1,0:T(8,128)S(1)}, f32[8,512]{1,0:T(8,128)S(1)}, u32[]{:S(2)}, u32[]{:S(2)}) collective-permute-start(f32[8,512]{1,0:T(8,128)S(1)} %shard_map.102.refs_9_), channel_id=1, source_target_pairs={{0,8},{1,9},{8,0},{9,1},{2,10},{3,11},{10,2},{11,3},{4,12},{5,13},... | collective-permute-start | bytes 49160 | tf_op jit(solution)/shard_map/ppermute | solution.py:66
  62.8 1.2 collective-permute-done.8.refs_10_
  64.0 2.1 %collective-permute-done.9.refs_11_ = f32[8,512]{1,0:T(8,128)S(1)} collective-permute-done((f32[8,512]{1,0:T(8,128)S(1)}, f32[8,512]{1,0:T(8,128)S(1)}, u32[]{:S(2)}, u32[]{:S(2)}) %collective-permute-start.9) | collective-permute-done | bytes 16416 | tf_op jit(solution)/shard_map/ppermute | solution.py:66
  66.1 2.5 %shard_map.103 = (bf16[320,128]{1,0:T(8,128)(2,1)S(1)}, bf16[320,128]{1,0:T(8,128)(2,1)S(1)}, bf16[320,128]{1,0:T(8,128)(2,1)S(1)}, bf16[320,128]{1,0:T(8,128)(2,1)S(1)}, bf16[4,320,128]{2,1,0:T(8,128)(2,1)}) custom-call(bf16[4,320,128]{2,1,0:T(8,128)(2,1)S(1)} %all-to-all-done.refs_0_, bf16[128,128]{1,0:T(8,128)(2,1)S(1)} %copy-done.3, ...), custom_call_target="tpu_custom_call" | custom-call | tf_op jit(solution)/shard_map/pallas_call | solution.py:50
  68.6 7.3 %all-to-all-start.1 = ((bf16[4,320,128]{2,1,0:T(8,128)(2,1)}), bf16[4,320,128]{2,1,0:T(8,128)(2,1)S(1)}, u32[]{:S(2)}, u32[]{:S(2)}) async-start(bf16[4,320,128]{2,1,0:T(8,128)(2,1)} %get-tuple-element.38), calls=%async_computation.1 | async-start | bytes 655360 | tf_op jit(solution)/shard_map/all_to_all | solution.py:61
  75.9 0.2 copy.17
  76.4 2.5 %collective-permute-start.11 = (bf16[512,128]{1,0:T(8,128)(2,1)S(1)}, bf16[512,128]{1,0:T(8,128)(2,1)S(1)}, u32[]{:S(2)}, u32[]{:S(2)}) collective-permute-start(bf16[512,128]{1,0:T(8,128)(2,1)S(1)} %get-tuple-element.57), channel_id=1, source_target_pairs={{0,8},{8,0},{128,136},{136,128},{1,9},{9,1},{129,137},{137,129},{2... | collective-permute-start | bytes 393224 | tf_op jit(solution)/shard_map/ppermute | solution.py:66
  79.0 1.9 %collective-permute-start.12 = (bf16[512,128]{1,0:T(8,128)(2,1)S(1)}, bf16[512,128]{1,0:T(8,128)(2,1)S(1)}, u32[]{:S(2)}, u32[]{:S(2)}) collective-permute-start(bf16[512,128]{1,0:T(8,128)(2,1)S(1)} %get-tuple-element.56), channel_id=1, source_target_pairs={{0,128},{8,136},{128,0},{136,8},{1,129},{9,137},{129,1},{137,9},{2... | collective-permute-start | bytes 393224 | tf_op jit(solution)/shard_map/ppermute | solution.py:66
  80.9 3.4 %collective-permute-start.13 = (bf16[512,128]{1,0:T(8,128)(2,1)S(1)}, bf16[512,128]{1,0:T(8,128)(2,1)S(1)}, u32[]{:S(2)}, u32[]{:S(2)}) collective-permute-start(bf16[512,128]{1,0:T(8,128)(2,1)S(1)} %get-tuple-element.55), channel_id=1, source_target_pairs={{0,136},{8,128},{128,8},{136,0},{1,137},{9,129},{129,9},{137,1},{2... | collective-permute-start | bytes 393224 | tf_op jit(solution)/shard_map/ppermute | solution.py:66
  84.3 3.8 %collective-permute-start.14 = (bf16[320,128]{1,0:T(8,128)(2,1)S(1)}, bf16[320,128]{1,0:T(8,128)(2,1)S(1)}, u32[]{:S(2)}, u32[]{:S(2)}) collective-permute-start(bf16[320,128]{1,0:T(8,128)(2,1)S(1)} %get-tuple-element.42), channel_id=1, source_target_pairs={{0,1},{1,0},{8,9},{9,8},{2,3},{3,2},{10,11},{11,10},{4,5},{5,4},{1... | collective-permute-start | bytes 245768 | tf_op jit(solution)/shard_map/ppermute | solution.py:66
  88.1 2.1 %collective-permute-start.15 = (bf16[320,128]{1,0:T(8,128)(2,1)S(1)}, bf16[320,128]{1,0:T(8,128)(2,1)S(1)}, u32[]{:S(2)}, u32[]{:S(2)}) collective-permute-start(bf16[320,128]{1,0:T(8,128)(2,1)S(1)} %get-tuple-element.43), channel_id=1, source_target_pairs={{0,8},{1,9},{8,0},{9,1},{2,10},{3,11},{10,2},{11,3},{4,12},{5,13},... | collective-permute-start | bytes 245768 | tf_op jit(solution)/shard_map/ppermute | solution.py:66
  90.3 3.5 %collective-permute-start.16 = (bf16[320,128]{1,0:T(8,128)(2,1)S(1)}, bf16[320,128]{1,0:T(8,128)(2,1)S(1)}, u32[]{:S(2)}, u32[]{:S(2)}) collective-permute-start(bf16[320,128]{1,0:T(8,128)(2,1)S(1)} %get-tuple-element.44), channel_id=1, source_target_pairs={{0,9},{1,8},{8,1},{9,0},{2,11},{3,10},{10,3},{11,2},{4,13},{5,12},... | collective-permute-start | bytes 245768 | tf_op jit(solution)/shard_map/ppermute | solution.py:66
  93.7 1.3 copy.19.refs_3_
  95.1 2.5 %collective-permute-done.16.refs_7_ = bf16[320,128]{1,0:T(8,128)(2,1)S(1)} collective-permute-done((bf16[320,128]{1,0:T(8,128)(2,1)S(1)}, bf16[320,128]{1,0:T(8,128)(2,1)S(1)}, u32[]{:S(2)}, u32[]{:S(2)}) %collective-permute-start.16) | collective-permute-done | bytes 81952 | tf_op jit(solution)/shard_map/ppermute | solution.py:66
  97.6 1.3 shard_map.104
  99.0 7.5 %all-to-all-start.2 = ((bf16[8,192,128]{2,1,0:T(8,128)(2,1)}), bf16[8,192,128]{2,1,0:T(8,128)(2,1)S(1)}, u32[]{:S(2)}, u32[]{:S(2)}) async-start(bf16[8,192,128]{2,1,0:T(8,128)(2,1)} %bitcast.15), calls=%async_computation.2 | async-start | bytes 786432 | tf_op jit(solution)/shard_map/all_to_all | solution.py:61
  106.4 2.4 %collective-permute-start.19 = (bf16[448,128]{1,0:T(8,128)(2,1)S(1)}, bf16[448,128]{1,0:T(8,128)(2,1)S(1)}, u32[]{:S(2)}, u32[]{:S(2)}) collective-permute-start(bf16[448,128]{1,0:T(8,128)(2,1)S(1)} %get-tuple-element.51.refs_4_), channel_id=1, source_target_pairs={{0,8},{8,0},{128,136},{136,128},{1,9},{9,1},{129,137},{137,129},{2... | collective-permute-start | bytes 344072 | tf_op jit(solution)/shard_map/ppermute | solution.py:66
  108.9 1.9 %collective-permute-start.20 = (bf16[448,128]{1,0:T(8,128)(2,1)S(1)}, bf16[448,128]{1,0:T(8,128)(2,1)S(1)}, u32[]{:S(2)}, u32[]{:S(2)}) collective-permute-start(bf16[448,128]{1,0:T(8,128)(2,1)S(1)} %get-tuple-element.51.refs_4_), channel_id=1, source_target_pairs={{0,128},{8,136},{128,0},{136,8},{1,129},{9,137},{129,1},{137,9},{2... | collective-permute-start | bytes 344072 | tf_op jit(solution)/shard_map/ppermute | solution.py:66
  110.8 3.5 %collective-permute-start.21 = (bf16[448,128]{1,0:T(8,128)(2,1)S(1)}, bf16[448,128]{1,0:T(8,128)(2,1)S(1)}, u32[]{:S(2)}, u32[]{:S(2)}) collective-permute-start(bf16[448,128]{1,0:T(8,128)(2,1)S(1)} %get-tuple-element.51.refs_4_), channel_id=1, source_target_pairs={{0,136},{8,128},{128,8},{136,0},{1,137},{9,129},{129,9},{137,1},{2... | collective-permute-start | bytes 344072 | tf_op jit(solution)/shard_map/ppermute | solution.py:66
  114.3 3.1 %collective-permute-done.21.refs_7_ = bf16[448,128]{1,0:T(8,128)(2,1)S(1)} collective-permute-done((bf16[448,128]{1,0:T(8,128)(2,1)S(1)}, bf16[448,128]{1,0:T(8,128)(2,1)S(1)}, u32[]{:S(2)}, u32[]{:S(2)}) %collective-permute-start.21) | collective-permute-done | bytes 114720 | tf_op jit(solution)/shard_map/ppermute | solution.py:66
  117.5 1.5 shard_map.107
  119.0 0.6 all-to-all-done.2.refs_0_
  119.6 12.3 %all-to-all-start.3 = ((bf16[32,16,448]{2,1,0:T(8,128)(2,1)}), bf16[32,16,448]{2,1,0:T(8,128)(2,1)S(1)}, u32[]{:S(2)}, u32[]{:S(2)}) async-start(bf16[32,16,448]{2,1,0:T(8,128)(2,1)} %bitcast.19), calls=%async_computation.3 | async-start | bytes 1048576 | tf_op jit(solution)/shard_map/all_to_all | solution.py:61
  131.9 3.4 %collective-permute-start.17 = (bf16[192,128]{1,0:T(8,128)(2,1)S(1)}, bf16[192,128]{1,0:T(8,128)(2,1)S(1)}, u32[]{:S(2)}, u32[]{:S(2)}) collective-permute-start(bf16[192,128]{1,0:T(8,128)(2,1)S(1)} %shard_map.105.refs_0_), channel_id=1, source_target_pairs={{0,1},{1,2},{2,3},{3,4},{4,5},{5,6},{6,7},{7,8},{8,9},{9,10},{10,1... | collective-permute-start | bytes 147464 | tf_op jit(solution)/shard_map/ppermute | solution.py:81
  135.3 2.5 %collective-permute-start.18 = (bf16[192,128]{1,0:T(8,128)(2,1)S(1)}, bf16[192,128]{1,0:T(8,128)(2,1)S(1)}, u32[]{:S(2)}, u32[]{:S(2)}) collective-permute-start(bf16[192,128]{1,0:T(8,128)(2,1)S(1)} %shard_map.105.refs_0_), channel_id=1, source_target_pairs={{1,0},{2,1},{3,2},{4,3},{5,4},{6,5},{7,6},{8,7},{9,8},{10,9},{11,1... | collective-permute-start | bytes 147464 | tf_op jit(solution)/shard_map/ppermute | solution.py:81
  137.8 0.8 constant_dynamic-slice_fusion
  138.7 0.5 collective-permute-done.17.refs_1_
  139.3 2.7 %collective-permute-done.18.refs_2_ = bf16[192,128]{1,0:T(8,128)(2,1)S(1)} collective-permute-done((bf16[192,128]{1,0:T(8,128)(2,1)S(1)}, bf16[192,128]{1,0:T(8,128)(2,1)S(1)}, u32[]{:S(2)}, u32[]{:S(2)}) %collective-permute-start.18) | collective-permute-done | bytes 49184 | tf_op jit(solution)/shard_map/ppermute | solution.py:81
  141.9 1.2 shard_map.106
  143.2 9.8 %all-to-all-done.3.refs_0_ = bf16[32,16,448]{2,1,0:T(8,128)(2,1)S(1)} async-done(((bf16[32,16,448]{2,1,0:T(8,128)(2,1)}), bf16[32,16,448]{2,1,0:T(8,128)(2,1)S(1)}, u32[]{:S(2)}, u32[]{:S(2)}) %all-to-all-start.3) | async-done | bytes 458784 | tf_op jit(solution)/shard_map/all_to_all | solution.py:61
  152.9 0.7 shard_map.108
  (35 shorter events, 0.6 us)
Async XLA Ops:
  0.6 28.6 %collective-permute-start.2 = (bf16[192,128]{1,0:T(8,128)(2,1)}, bf16[192,128]{1,0:T(8,128)(2,1)S(1)}, u32[]{:S(2)}, u32[]{:S(2)}) collective-permute-start(bf16[192,128]{1,0:T(8,128)(2,1)} %bitcast.32), channel_id=1, source_target_pairs={{0,1},{1,0},{8,9},{9,8},{2,3},{3,2},{10,11},{11,10},{4,5},{5,4},{1... | collective-permute-start | bytes 147464 | tf_op jit(solution)/shard_map/ppermute | solution.py:66
  15.5 13.7 %collective-permute-start.3 = (bf16[192,128]{1,0:T(8,128)(2,1)}, bf16[192,128]{1,0:T(8,128)(2,1)S(1)}, u32[]{:S(2)}, u32[]{:S(2)}) collective-permute-start(bf16[192,128]{1,0:T(8,128)(2,1)} %bitcast.33), channel_id=1, source_target_pairs={{0,8},{1,9},{8,0},{9,1},{2,10},{3,11},{10,2},{11,3},{4,12},{5,13},... | collective-permute-start | bytes 147464 | tf_op jit(solution)/shard_map/ppermute | solution.py:66
  17.4 11.8 %collective-permute-start.4 = (bf16[192,128]{1,0:T(8,128)(2,1)}, bf16[192,128]{1,0:T(8,128)(2,1)S(1)}, u32[]{:S(2)}, u32[]{:S(2)}) collective-permute-start(bf16[192,128]{1,0:T(8,128)(2,1)} %bitcast.34), channel_id=1, source_target_pairs={{0,9},{1,8},{8,1},{9,0},{2,11},{3,10},{10,3},{11,2},{4,13},{5,12},... | collective-permute-start | bytes 147464 | tf_op jit(solution)/shard_map/ppermute | solution.py:66
  21.6 5.8 %collective-permute-start = (bf16[8,1536]{1,0:T(8,128)(2,1)S(1)}, bf16[8,1536]{1,0:T(8,128)(2,1)S(1)}, u32[]{:S(2)}, u32[]{:S(2)}) collective-permute-start(bf16[8,1536]{1,0:T(8,128)(2,1)S(1)} %get-tuple-element.60), channel_id=1, source_target_pairs={{0,1},{1,2},{2,3},{3,4},{4,5},{5,6},{6,7},{7,8},{8,9},{9,10},{10,1... | collective-permute-start | bytes 73736 | tf_op jit(solution)/shard_map/ppermute | solution.py:81
  23.5 5.7 %collective-permute-start.1 = (bf16[8,1536]{1,0:T(8,128)(2,1)S(1)}, bf16[8,1536]{1,0:T(8,128)(2,1)S(1)}, u32[]{:S(2)}, u32[]{:S(2)}) collective-permute-start(bf16[8,1536]{1,0:T(8,128)(2,1)S(1)} %get-tuple-element.59), channel_id=1, source_target_pairs={{1,0},{2,1},{3,2},{4,3},{5,4},{6,5},{7,6},{8,7},{9,8},{10,9},{11,1... | collective-permute-start | bytes 73736 | tf_op jit(solution)/shard_map/ppermute | solution.py:81
  27.4 1.8 %copy-start.5 = (bf16[8,1536]{1,0:T(8,128)(2,1)}, bf16[8,1536]{1,0:T(8,128)(2,1)S(1)}, u32[]{:S(2)}) copy-start(bf16[8,1536]{1,0:T(8,128)(2,1)S(1)} %collective-permute-done.refs_4_) | copy-start | bytes 73732
  29.2 0.6 copy-start.6
  33.9 7.9 %copy-start.3 = (bf16[128,128]{1,0:T(8,128)(2,1)S(1)}, bf16[128,128]{1,0:T(8,128)(2,1)}, u32[]{:S(2)}) copy-start(bf16[128,128]{1,0:T(8,128)(2,1)} %get-tuple-element.33.refs_1_) | copy-start | bytes 98308
  33.9 19.0 %copy-start.2 = (bf16[1,128,192]{1,2,0:T(8,128)(2,1)S(1)}, bf16[1,128,192]{1,2,0:T(8,128)(2,1)}, u32[]{:S(2)}) copy-start(bf16[1,128,192]{1,2,0:T(8,128)(2,1)} %param.11) | copy-start | bytes 147460
  33.9 19.0 %all-to-all-start = ((bf16[4,320,128]{2,1,0:T(8,128)(2,1)}), bf16[4,320,128]{2,1,0:T(8,128)(2,1)S(1)}, u32[]{:S(2)}, u32[]{:S(2)}) async-start(bf16[4,320,128]{2,1,0:T(8,128)(2,1)} %get-tuple-element.32), calls=%async_computation | async-start | bytes 655360 | tf_op jit(solution)/shard_map/all_to_all | solution.py:61
  41.8 9.2 %collective-permute-start.5 = (bf16[128,128]{1,0:T(8,128)(2,1)S(1)}, bf16[128,128]{1,0:T(8,128)(2,1)S(1)}, u32[]{:S(2)}, u32[]{:S(2)}) collective-permute-start(bf16[128,128]{1,0:T(8,128)(2,1)S(1)} %copy-done.3), channel_id=1, source_target_pairs={{0,1},{1,0},{8,9},{9,8},{2,3},{3,2},{10,11},{11,10},{4,5},{5,4},{1... | collective-permute-start | bytes 98312 | tf_op jit(solution)/shard_map/ppermute | solution.py:66
  43.7 7.3 %collective-permute-start.6 = (bf16[128,128]{1,0:T(8,128)(2,1)S(1)}, bf16[128,128]{1,0:T(8,128)(2,1)S(1)}, u32[]{:S(2)}, u32[]{:S(2)}) collective-permute-start(bf16[128,128]{1,0:T(8,128)(2,1)S(1)} %copy-done.3), channel_id=1, source_target_pairs={{0,8},{1,9},{8,0},{9,1},{2,10},{3,11},{10,2},{11,3},{4,12},{5,13},... | collective-permute-start | bytes 98312 | tf_op jit(solution)/shard_map/ppermute | solution.py:66
  45.7 7.3 %collective-permute-start.7 = (bf16[128,128]{1,0:T(8,128)(2,1)S(1)}, bf16[128,128]{1,0:T(8,128)(2,1)S(1)}, u32[]{:S(2)}, u32[]{:S(2)}) collective-permute-start(bf16[128,128]{1,0:T(8,128)(2,1)S(1)} %copy-done.3), channel_id=1, source_target_pairs={{0,9},{1,8},{8,1},{9,0},{2,11},{3,10},{10,3},{11,2},{4,13},{5,12},... | collective-permute-start | bytes 98312 | tf_op jit(solution)/shard_map/ppermute | solution.py:66
  53.6 9.2 %collective-permute-start.10 = (f32[8,512]{1,0:T(8,128)S(1)}, f32[8,512]{1,0:T(8,128)S(1)}, u32[]{:S(2)}, u32[]{:S(2)}) collective-permute-start(f32[8,512]{1,0:T(8,128)S(1)} %shard_map.102.refs_9_), channel_id=1, source_target_pairs={{0,9},{1,8},{8,1},{9,0},{2,11},{3,10},{10,3},{11,2},{4,13},{5,12},... | collective-permute-start | bytes 49160 | tf_op jit(solution)/shard_map/ppermute | solution.py:66
  58.4 5.6 %collective-permute-start.8 = (f32[8,512]{1,0:T(8,128)S(1)}, f32[8,512]{1,0:T(8,128)S(1)}, u32[]{:S(2)}, u32[]{:S(2)}) collective-permute-start(f32[8,512]{1,0:T(8,128)S(1)} %shard_map.102.refs_9_), channel_id=1, source_target_pairs={{0,1},{1,0},{8,9},{9,8},{2,3},{3,2},{10,11},{11,10},{4,5},{5,4},{1... | collective-permute-start | bytes 49160 | tf_op jit(solution)/shard_map/ppermute | solution.py:66
  60.3 5.8 %collective-permute-start.9 = (f32[8,512]{1,0:T(8,128)S(1)}, f32[8,512]{1,0:T(8,128)S(1)}, u32[]{:S(2)}, u32[]{:S(2)}) collective-permute-start(f32[8,512]{1,0:T(8,128)S(1)} %shard_map.102.refs_9_), channel_id=1, source_target_pairs={{0,8},{1,9},{8,0},{9,1},{2,10},{3,11},{10,2},{11,3},{4,12},{5,13},... | collective-permute-start | bytes 49160 | tf_op jit(solution)/shard_map/ppermute | solution.py:66
  68.6 7.3 %copy-start.4 = (bf16[128,1536]{1,0:T(8,128)(2,1)S(1)}, bf16[128,1536]{1,0:T(8,128)(2,1)}, u32[]{:S(2)}) copy-start(bf16[128,1536]{1,0:T(8,128)(2,1)} %get-tuple-element.39) | copy-start | bytes 1179652
  68.6 26.5 %all-to-all-start.1 = ((bf16[4,320,128]{2,1,0:T(8,128)(2,1)}), bf16[4,320,128]{2,1,0:T(8,128)(2,1)S(1)}, u32[]{:S(2)}, u32[]{:S(2)}) async-start(bf16[4,320,128]{2,1,0:T(8,128)(2,1)} %get-tuple-element.38), calls=%async_computation.1 | async-start | bytes 655360 | tf_op jit(solution)/shard_map/all_to_all | solution.py:61
  76.4 13.8 %collective-permute-start.11 = (bf16[512,128]{1,0:T(8,128)(2,1)S(1)}, bf16[512,128]{1,0:T(8,128)(2,1)S(1)}, u32[]{:S(2)}, u32[]{:S(2)}) collective-permute-start(bf16[512,128]{1,0:T(8,128)(2,1)S(1)} %get-tuple-element.57), channel_id=1, source_target_pairs={{0,8},{8,0},{128,136},{136,128},{1,9},{9,1},{129,137},{137,129},{2... | collective-permute-start | bytes 393224 | tf_op jit(solution)/shard_map/ppermute | solution.py:66
  79.0 16.1 %collective-permute-start.12 = (bf16[512,128]{1,0:T(8,128)(2,1)S(1)}, bf16[512,128]{1,0:T(8,128)(2,1)S(1)}, u32[]{:S(2)}, u32[]{:S(2)}) collective-permute-start(bf16[512,128]{1,0:T(8,128)(2,1)S(1)} %get-tuple-element.56), channel_id=1, source_target_pairs={{0,128},{8,136},{128,0},{136,8},{1,129},{9,137},{129,1},{137,9},{2... | collective-permute-start | bytes 393224 | tf_op jit(solution)/shard_map/ppermute | solution.py:66
  80.9 14.2 %collective-permute-start.13 = (bf16[512,128]{1,0:T(8,128)(2,1)S(1)}, bf16[512,128]{1,0:T(8,128)(2,1)S(1)}, u32[]{:S(2)}, u32[]{:S(2)}) collective-permute-start(bf16[512,128]{1,0:T(8,128)(2,1)S(1)} %get-tuple-element.55), channel_id=1, source_target_pairs={{0,136},{8,128},{128,8},{136,0},{1,137},{9,129},{129,9},{137,1},{2... | collective-permute-start | bytes 393224 | tf_op jit(solution)/shard_map/ppermute | solution.py:66
  84.3 10.8 %collective-permute-start.14 = (bf16[320,128]{1,0:T(8,128)(2,1)S(1)}, bf16[320,128]{1,0:T(8,128)(2,1)S(1)}, u32[]{:S(2)}, u32[]{:S(2)}) collective-permute-start(bf16[320,128]{1,0:T(8,128)(2,1)S(1)} %get-tuple-element.42), channel_id=1, source_target_pairs={{0,1},{1,0},{8,9},{9,8},{2,3},{3,2},{10,11},{11,10},{4,5},{5,4},{1... | collective-permute-start | bytes 245768 | tf_op jit(solution)/shard_map/ppermute | solution.py:66
  88.1 7.0 %collective-permute-start.15 = (bf16[320,128]{1,0:T(8,128)(2,1)S(1)}, bf16[320,128]{1,0:T(8,128)(2,1)S(1)}, u32[]{:S(2)}, u32[]{:S(2)}) collective-permute-start(bf16[320,128]{1,0:T(8,128)(2,1)S(1)} %get-tuple-element.43), channel_id=1, source_target_pairs={{0,8},{1,9},{8,0},{9,1},{2,10},{3,11},{10,2},{11,3},{4,12},{5,13},... | collective-permute-start | bytes 245768 | tf_op jit(solution)/shard_map/ppermute | solution.py:66
  90.2 7.4 %copy-start = (bf16[1536,128]{1,0:T(8,128)(2,1)S(1)}, bf16[1536,128]{1,0:T(8,128)(2,1)}, u32[]{:S(2)}) copy-start(bf16[1536,128]{1,0:T(8,128)(2,1)} %refs_1_.3) | copy-start | bytes 1179652
  90.2 7.4 %copy-start.1 = (bf16[1536,128]{1,0:T(8,128)(2,1)S(1)}, bf16[1536,128]{1,0:T(8,128)(2,1)}, u32[]{:S(2)}) copy-start(bf16[1536,128]{1,0:T(8,128)(2,1)} %refs_2_.3) | copy-start | bytes 1179652
  90.3 7.4 %collective-permute-start.16 = (bf16[320,128]{1,0:T(8,128)(2,1)S(1)}, bf16[320,128]{1,0:T(8,128)(2,1)S(1)}, u32[]{:S(2)}, u32[]{:S(2)}) collective-permute-start(bf16[320,128]{1,0:T(8,128)(2,1)S(1)} %get-tuple-element.44), channel_id=1, source_target_pairs={{0,9},{1,8},{8,1},{9,0},{2,11},{3,10},{10,3},{11,2},{4,13},{5,12},... | collective-permute-start | bytes 245768 | tf_op jit(solution)/shard_map/ppermute | solution.py:66
  99.0 20.6 %all-to-all-start.2 = ((bf16[8,192,128]{2,1,0:T(8,128)(2,1)}), bf16[8,192,128]{2,1,0:T(8,128)(2,1)S(1)}, u32[]{:S(2)}, u32[]{:S(2)}) async-start(bf16[8,192,128]{2,1,0:T(8,128)(2,1)} %bitcast.15), calls=%async_computation.2 | async-start | bytes 786432 | tf_op jit(solution)/shard_map/all_to_all | solution.py:61
  106.4 7.9 %collective-permute-start.19 = (bf16[448,128]{1,0:T(8,128)(2,1)S(1)}, bf16[448,128]{1,0:T(8,128)(2,1)S(1)}, u32[]{:S(2)}, u32[]{:S(2)}) collective-permute-start(bf16[448,128]{1,0:T(8,128)(2,1)S(1)} %get-tuple-element.51.refs_4_), channel_id=1, source_target_pairs={{0,8},{8,0},{128,136},{136,128},{1,9},{9,1},{129,137},{137,129},{2... | collective-permute-start | bytes 344072 | tf_op jit(solution)/shard_map/ppermute | solution.py:66
  108.9 5.5 %collective-permute-start.20 = (bf16[448,128]{1,0:T(8,128)(2,1)S(1)}, bf16[448,128]{1,0:T(8,128)(2,1)S(1)}, u32[]{:S(2)}, u32[]{:S(2)}) collective-permute-start(bf16[448,128]{1,0:T(8,128)(2,1)S(1)} %get-tuple-element.51.refs_4_), channel_id=1, source_target_pairs={{0,128},{8,136},{128,0},{136,8},{1,129},{9,137},{129,1},{137,9},{2... | collective-permute-start | bytes 344072 | tf_op jit(solution)/shard_map/ppermute | solution.py:66
  110.8 6.7 %collective-permute-start.21 = (bf16[448,128]{1,0:T(8,128)(2,1)S(1)}, bf16[448,128]{1,0:T(8,128)(2,1)S(1)}, u32[]{:S(2)}, u32[]{:S(2)}) collective-permute-start(bf16[448,128]{1,0:T(8,128)(2,1)S(1)} %get-tuple-element.51.refs_4_), channel_id=1, source_target_pairs={{0,136},{8,128},{128,8},{136,0},{1,137},{9,129},{129,9},{137,1},{2... | collective-permute-start | bytes 344072 | tf_op jit(solution)/shard_map/ppermute | solution.py:66
  119.6 33.3 %all-to-all-start.3 = ((bf16[32,16,448]{2,1,0:T(8,128)(2,1)}), bf16[32,16,448]{2,1,0:T(8,128)(2,1)S(1)}, u32[]{:S(2)}, u32[]{:S(2)}) async-start(bf16[32,16,448]{2,1,0:T(8,128)(2,1)} %bitcast.19), calls=%async_computation.3 | async-start | bytes 1048576 | tf_op jit(solution)/shard_map/all_to_all | solution.py:61
  131.9 7.3 %collective-permute-start.17 = (bf16[192,128]{1,0:T(8,128)(2,1)S(1)}, bf16[192,128]{1,0:T(8,128)(2,1)S(1)}, u32[]{:S(2)}, u32[]{:S(2)}) collective-permute-start(bf16[192,128]{1,0:T(8,128)(2,1)S(1)} %shard_map.105.refs_0_), channel_id=1, source_target_pairs={{0,1},{1,2},{2,3},{3,4},{4,5},{5,6},{6,7},{7,8},{8,9},{9,10},{10,1... | collective-permute-start | bytes 147464 | tf_op jit(solution)/shard_map/ppermute | solution.py:81
  135.3 6.6 %collective-permute-start.18 = (bf16[192,128]{1,0:T(8,128)(2,1)S(1)}, bf16[192,128]{1,0:T(8,128)(2,1)S(1)}, u32[]{:S(2)}, u32[]{:S(2)}) collective-permute-start(bf16[192,128]{1,0:T(8,128)(2,1)S(1)} %shard_map.105.refs_0_), channel_id=1, source_target_pairs={{1,0},{2,1},{3,2},{4,3},{5,4},{6,5},{7,6},{8,7},{9,8},{10,9},{11,1... | collective-permute-start | bytes 147464 | tf_op jit(solution)/shard_map/ppermute | solution.py:81
